TPU v7x, 32 devices: a whole 2x2x4 slice. The times are simulated.
32 devices in a mesh: ctx: 8 (over y, x, core), ch: 4 (over z).
Axes of the slice: x: 2, y: 2, z: 4, core: 2. Of those that a mesh axis runs over, the one named last changes fastest.
Arguments:
- queries: bfloat16 [8192, 2048], P('ch', 'ctx'), may hold values from -6 to 6
- keys: bfloat16 [8192, 2048], P('ch', 'ctx'), may hold values from -6 to 6
- values: bfloat16 [8192, 2048], P('ch', 'ctx'), may hold values from -6 to 6
- short_taps: float32 [3, 7, 8192], P(None, None, 'ch'), may hold values from -2 to 2
- long_filter: bfloat16 [4, 2048, 2048], P('ch', 'ctx'), may hold values from -1.5 to 1.5
- skip_gain: float32 [4, 2048], P('ch', 'ctx'), may hold values from 0.5 to 1.5
Outputs:
- mixed: bfloat16 [8192, 2048], P('ch', 'ctx')
All inputs are finite; a program needn't handle non-finite values.
Results may differ from a plain program's by a relative error of at most 0.01.
Values may be sent and summed in bfloat16 or wider, within the bound.
A program may use at most 64 MiB of HBM per device.

v0:
```python
import functools
import math

import jax
import jax.numpy as jnp
import ml_dtypes
import numpy as np
from jax import lax
from jax.experimental import pallas as pl
from jax.experimental.pallas import tpu as pltpu
from jax.sharding import PartitionSpec as P

MESH = pl.DeviceIdType.MESH
LANES = 128
SLOT = 8
F32 = jnp.float32
BF16 = jnp.bfloat16


def leaf_angles(count, theta):
    if count == 1:
        return [theta]
    return leaf_angles(count // 2, theta / 2) + leaf_angles(count // 2, theta / 2 + math.pi)


def circle_tables():
    place = np.arange(LANES, dtype=np.float64)
    angle = place[:, None] * place[None, :] * (2.0 * math.pi / LANES)
    cos, sin = np.cos(angle), np.sin(angle)
    there = np.block([[cos, -sin], [sin, cos]])
    return np.stack([there, there.T]).astype(ml_dtypes.bfloat16)


def twist_columns(count):
    roots = np.array(leaf_angles(count, 0.0)) + math.pi / (2 * count)
    angle = np.arange(LANES)[:, None] * roots[None, :] / LANES
    return np.concatenate([np.cos(angle), np.sin(angle)], axis=1).astype(np.float32)


def turn(re, im, angle):
    eighth = round(angle / (math.pi / 4))
    if abs(angle - eighth * math.pi / 4) > 1e-9:
        cos, sin = math.cos(angle), math.sin(angle)
        return cos * re - sin * im, cos * im + sin * re
    eighth %= 8
    if eighth % 2:
        re, im = math.sqrt(0.5) * (re - im), math.sqrt(0.5) * (re + im)
    return [(re, im), (-im, re), (-re, -im), (im, -re)][eighth // 2]


def split_forward(coefs, theta, first, emit):
    count = len(coefs)
    if count == 1:
        emit(first, *coefs[0])
        return
    half = count // 2
    plus, minus = [], []
    for (lo_re, lo_im), high in zip(coefs[:half], coefs[half:]):
        hi_re, hi_im = turn(*high, theta / 2)
        plus.append((lo_re + hi_re, lo_im + hi_im))
        minus.append((lo_re - hi_re, lo_im - hi_im))
    split_forward(plus, theta / 2, first, emit)
    split_forward(minus, theta / 2 + math.pi, first + half, emit)


def split_inverse(fetch, count, theta, first):
    if count == 1:
        return [fetch(first)]
    half = count // 2
    plus = split_inverse(fetch, half, theta / 2, first)
    minus = split_inverse(fetch, half, theta / 2 + math.pi, first + half)
    low, high = [], []
    for (p_re, p_im), (m_re, m_im) in zip(plus, minus):
        low.append((p_re + m_re, p_im + m_im))
        high.append(turn(p_re - m_re, p_im - m_im, -theta / 2))
    return low + high


def across(eye, block):
    return lax.dot_general(eye, block, (((1,), (1,)), ((), ())), preferred_element_type=F32)


def kernel(
    n, lanes,
    q_ref, k_ref, v_ref, taps_ref, filt_hbm, gain_ref, table_ref, twist_ref,
    out_hbm,
    out_ref, eye, tails, halo, turned, gated, recv, spec, h_spec, ret, filt_ref, filt_rows, twist,
    filt_sem, halo_sem, in_send, in_recv, in_own, out_send, out_recv, out_own, put,
):
    me = lax.axis_index("ctx")
    width, tok = q_ref.shape
    chan, length = filt_ref.shape
    chunks = chan // lanes
    rim = taps_ref.shape[-2]
    blocks = length // LANES
    tiles = tok // LANES
    sources = (q_ref, k_ref, v_ref)
    step = 16
    filt_copy = pltpu.make_async_copy(filt_hbm, filt_ref, filt_sem)
    filt_copy.start()

    barrier = pltpu.get_barrier_semaphore()
    for d in range(1, n):
        pl.semaphore_signal(barrier, inc=1, device_id={"ctx": lax.rem(me + d, n)}, device_id_type=MESH)

    side = eye.shape[0]
    row = lax.broadcasted_iota(jnp.int32, (side, side), 0)
    col = lax.broadcasted_iota(jnp.int32, (side, side), 1)
    eye[...] = (row == col).astype(F32).astype(BF16)

    pick_row = lax.broadcasted_iota(jnp.int32, (SLOT, LANES), 0) + (LANES - SLOT)
    pick = (pick_row == lax.broadcasted_iota(jnp.int32, (SLOT, LANES), 1)).astype(F32).astype(BF16)

    def tail_step(p, _):
        at = pl.ds(pl.multiple_of(p * chan, chan), chan)
        for w in range(3):
            tails[w, p] = across(pick, sources[w][at, tok - LANES :]).astype(BF16)
        return 0

    lax.fori_loop(0, n, tail_step, 0, unroll=4)

    pl.semaphore_wait(barrier, n - 1)
    halo_copy = pltpu.make_async_remote_copy(
        src_ref=tails, dst_ref=halo, send_sem=halo_sem.at[0], recv_sem=halo_sem.at[1],
        device_id={"ctx": lax.rem(me + 1, n)}, device_id_type=MESH,
    )

    halo_copy.start()
    if lanes < LANES:
        spec[...] = jnp.zeros_like(spec)

    filt_copy.wait()
    for a in range(blocks):
        filt_rows[a // tiles, (a % tiles) * LANES : (a % tiles + 1) * LANES, :] = across(
            eye[:LANES, :LANES], filt_ref[:, a * LANES : (a + 1) * LANES]
        ).astype(BF16)

    def chunk_lanes(c):
        return slice(c * lanes, (c + 1) * lanes)

    def leaf_lanes(leaf):
        return slice((leaf % 2) * LANES, (leaf % 2) * LANES + lanes)

    def short_stage(ref, c, first=False):
        at_lanes = chunk_lanes(c)

        def one(r, _):
            re_at = pl.ds(pl.multiple_of(r * step, step), step)
            im_at = pl.ds(pl.multiple_of(LANES + r * step, step), step)

            def emit(leaf, re, im):
                if first:
                    for which in range(2):
                        column = twist_ref[re_at, which * blocks + leaf : which * blocks + leaf + 1]
                        twist[leaf, which, re_at, :] = jnp.broadcast_to(column, (step, lanes))
                cos, sin = twist[leaf, 0, re_at, :], twist[leaf, 1, re_at, :]
                spec[leaf // 2, re_at, leaf_lanes(leaf)] = (re * cos - im * sin).astype(BF16)
                spec[leaf // 2, im_at, leaf_lanes(leaf)] = (re * sin + im * cos).astype(BF16)

            coefs = []
            for a in range(blocks):
                at = pl.ds(pl.multiple_of((a % tiles) * LANES + r * step, step), step)
                x, lean = ref[a // tiles, at, at_lanes].astype(F32), a * math.pi / (2 * blocks)
                coefs.append((x * math.cos(lean), x * math.sin(lean)))
            split_forward(coefs, 0.0, 0, emit)
            return 0

        lax.fori_loop(0, LANES // step, one, 0)

    def filter_chunk(c):
        short_stage(filt_rows, c, c == 0)

        def filt_pair(pair, _):
            h_spec[c, pair] = jnp.dot(table_ref[0], spec[pair], preferred_element_type=F32).astype(h_spec.dtype)
            return 0

        lax.fori_loop(0, blocks // 2, filt_pair, 0, unroll=2)

    filter_chunk(0)
    halo_copy.wait()

    def peer_rows(peer, c):
        return pl.ds(pl.multiple_of(peer * chan + c * lanes, lanes), lanes)

    def short(first, pair, c):
        block = jnp.concatenate([sources[w][peer_rows(peer, c), :] for w, peer in pair], axis=0)
        both = across(eye[:tok, :tok], block)
        taps = []
        for i, (w, peer) in enumerate(pair):
            turned[first + i, :SLOT, :] = jnp.where(me > 0, halo[w, peer, :, chunk_lanes(c)].astype(F32), 0.0)
            turned[first + i, SLOT:, :] = both[:, i * lanes : (i + 1) * lanes]
            if len(taps_ref.shape) == 3:
                taps.append(taps_ref[w, :, peer_rows(peer, c)])
            else:
                taps.append(taps_ref[peer, w, :, chunk_lanes(c)])
        return taps

    def sums_of(slot, taps, start, count):
        total = None
        for j in range(rim):
            term = taps[j : j + 1, :] * turned[slot, SLOT - j + start : SLOT - j + start + count, :]
            total = term if total is None else total + term
        return total

    part = 64

    def gate_pair(peers, c):
        taps = [short(2 * i, [(1, p), (2, p)], c) for i, p in enumerate(peers)]
        for i, p in enumerate(peers):
            for start in range(0, tok, part):
                product = sums_of(2 * i, taps[i][0], start, part) * sums_of(2 * i + 1, taps[i][1], start, part)
                gated[p, start : start + part, chunk_lanes(c)] = product.astype(BF16)

    def in_copy(c, d):
        peer = lax.rem(me + d, n)
        return pltpu.make_async_remote_copy(
            src_ref=gated.at[peer, :, chunk_lanes(c)], dst_ref=recv.at[me, :, chunk_lanes(c)],
            send_sem=in_send.at[c, d], recv_sem=in_recv.at[c, d],
            device_id={"ctx": peer}, device_id_type=MESH,
        )

    def own_in(c):
        return pltpu.make_async_copy(gated.at[me, :, chunk_lanes(c)], recv.at[me, :, chunk_lanes(c)], in_own.at[c])

    def out_copy(c, d):
        peer = lax.rem(me + d, n)
        return pltpu.make_async_remote_copy(
            src_ref=recv.at[peer, :, chunk_lanes(c)], dst_ref=ret.at[me, :, chunk_lanes(c)],
            send_sem=out_send.at[c, d], recv_sem=out_recv.at[c, d],
            device_id={"ctx": peer}, device_id_type=MESH,
        )

    def own_out(c):
        return pltpu.make_async_copy(recv.at[me, :, chunk_lanes(c)], ret.at[me, :, chunk_lanes(c)], out_own.at[c])

    for c in range(chunks):
        def send_step(i, _):
            gate_pair([lax.rem(me + 2 * i + 1, n), lax.rem(me + 2 * i + 2, n)], c)

            @pl.when(i > 0)
            def _():
                in_copy(c, 2 * i - 1).start()
                in_copy(c, 2 * i).start()

            return 0

        lax.fori_loop(0, n // 2, send_step, 0)
        in_copy(c, n - 1).start()
        own_in(c).start()

    for c in range(1, chunks):
        filter_chunk(c)

    for c in range(chunks):
        def wait_in(d, _):
            in_copy(c, d).wait()
            return 0

        lax.fori_loop(1, n, wait_in, 0)
        own_in(c).wait()
        at_lanes = chunk_lanes(c)
        short_stage(recv, c)

        def pair_step(pair, _):
            sig = jnp.dot(table_ref[0], spec[pair], preferred_element_type=F32)
            h_re, h_im = h_spec[c, pair, :LANES, :].astype(F32), h_spec[c, pair, LANES:, :].astype(F32)
            s_re, s_im = sig[:LANES], sig[LANES:]
            prod = jnp.concatenate([s_re * h_re - s_im * h_im, s_re * h_im + s_im * h_re], axis=0).astype(BF16)
            h_spec[c, pair] = jnp.dot(table_ref[1], prod, preferred_element_type=F32).astype(h_spec.dtype)
            return 0

        lax.fori_loop(0, blocks // 2, pair_step, 0, unroll=4)
        gain = gain_ref[:, at_lanes]

        def back_step(r, _):
            re_at = pl.ds(pl.multiple_of(r * step, step), step)
            im_at = pl.ds(pl.multiple_of(LANES + r * step, step), step)
            def fetch(leaf):
                re = h_spec[c, leaf // 2, re_at, leaf_lanes(leaf)].astype(F32)
                im = h_spec[c, leaf // 2, im_at, leaf_lanes(leaf)].astype(F32)
                cos, sin = twist[leaf, 0, re_at, :], twist[leaf, 1, re_at, :]
                return re * cos + im * sin, im * cos - re * sin

            parts = split_inverse(fetch, blocks, 0.0, 0)
            for a, (re, im) in enumerate(parts):
                lean = a * math.pi / (2 * blocks)
                cos, sin = math.cos(lean) / length, math.sin(lean) / length
                at = pl.ds(pl.multiple_of((a % tiles) * LANES + r * step, step), step)
                sig = recv[a // tiles, at, at_lanes].astype(F32)
                recv[a // tiles, at, at_lanes] = (cos * re + sin * im + gain * sig).astype(BF16)
            return 0

        lax.fori_loop(0, LANES // step, back_step, 0)

        def return_step(d, _):
            out_copy(c, d).start()
            return 0

        lax.fori_loop(1, n, return_step, 0)
        own_out(c).start()

    for c in range(chunks):
        def q_step(i, _):
            peers = (2 * i, 2 * i + 1)
            taps = short(0, [(0, p) for p in peers], c)
            for slot, p in enumerate(peers):
                parts = [sums_of(slot, taps[slot], start, part).astype(BF16) for start in range(0, tok, part)]
                out_ref[peer_rows(p, c), :] = across(eye[:lanes, :lanes], jnp.concatenate(parts, axis=0)).astype(BF16)
            return 0

        lax.fori_loop(0, n // 2, q_step, 0)

    def mix(peer, c):
        at = peer_rows(peer, c)
        long = across(eye[:lanes, :lanes], ret[peer, :, chunk_lanes(c)])
        out_ref[at, :] = (out_ref[at, :].astype(F32) * long).astype(BF16)
        put_copy(peer, c).start()

    def put_copy(peer, c):
        at = peer_rows(peer, c)
        return pltpu.make_async_copy(out_ref.at[at, :], out_hbm.at[at, :], put.at[c, peer])

    for c in range(chunks):
        own_out(c).wait()
        mix(me, c)

        def mix_step(d, _):
            out_copy(c, d).wait()
            mix(lax.rem(me + n - d, n), c)
            return 0

        lax.fori_loop(1, n, mix_step, 0)

    for c in range(chunks):
        def put_step(p, _):
            put_copy(p, c).wait()
            return 0

        lax.fori_loop(0, n, put_step, 0)


def solution(mesh):
    n = mesh.shape["ctx"]

    def local(queries, keys, values, short_taps, long_filter, skip_gain):
        width, tok = queries.shape
        chan, length = long_filter.shape[1:]
        blocks = length // LANES
        lanes = min(chan, LANES)
        chunks = chan // lanes
        table = jnp.asarray(circle_tables())
        twist = jnp.asarray(twist_columns(blocks))
        dma = pltpu.SemaphoreType.DMA
        two = 2 * LANES
        small = blocks * two * max(chan, LANES) * 4 <= 8 * 2**20
        side = max(tok, LANES)
        any_space = pl.BlockSpec(memory_space=pl.ANY)
        taps = short_taps
        if lanes < LANES:
            taps = jnp.moveaxis(short_taps.reshape(3, -1, n, chan), 2, 0)
        return pl.pallas_call(
            functools.partial(kernel, n, lanes),
            out_shape=jax.ShapeDtypeStruct((width, tok), BF16),
            in_specs=[any_space if i == 4 else pl.BlockSpec(memory_space=pltpu.VMEM) for i in range(8)],
            out_specs=any_space,
            scratch_shapes=[
                pltpu.VMEM((width, tok), BF16),
                pltpu.VMEM((side, side), BF16),
                pltpu.VMEM((3, n, SLOT, chan), BF16),
                pltpu.VMEM((3, n, SLOT, chan), BF16),
                pltpu.VMEM((4, SLOT + tok, lanes), F32),
                pltpu.VMEM((n, tok, chan), BF16),
                pltpu.VMEM((n, tok, chan), BF16),
                pltpu.VMEM((blocks // 2, two, two), BF16),
                pltpu.VMEM((chunks, blocks // 2, two, two), F32 if small else BF16),
                pltpu.VMEM((n, tok, chan), BF16),
                pltpu.VMEM((chan, length), BF16),
                pltpu.VMEM((n, tok, chan), BF16),
                pltpu.VMEM((blocks, 2, LANES, lanes), F32),
                dma,
                dma((2,)),
                dma((chunks, n)),
                dma((chunks, n)),
                dma((chunks,)),
                dma((chunks, n)),
                dma((chunks, n)),
                dma((chunks,)),
                dma((chunks, n)),
            ],
            compiler_params=pltpu.CompilerParams(
                collective_id=0, has_side_effects=True, vmem_limit_bytes=67043328
            ),
            name="hyena",
        )(queries, keys, values, taps, long_filter[0], skip_gain, table, twist)

    placed = (
        P("ch", "ctx"),
        P("ch", "ctx"),
        P("ch", "ctx"),
        P(None, None, "ch"),
        P("ch", "ctx", None),
        P("ch", "ctx"),
    )
    return jax.shard_map(local, mesh=mesh, in_specs=placed, out_specs=P("ch", "ctx"), check_vma=False)
```

profile of v0, /device:TPU:0, one launch (start us, length us, event | category | flops | bytes accessed | tf_op | source)
XLA Modules:
  0.0 37.8 jit_solution(17076653858419255266)
XLA Ops:
  0.0 35.6 %hyena.1 = bf16[2048,256]{1,0:T(8,128)(2,1)} custom-call(bf16[2048,256]{1,0:T(8,128)(2,1)} %q_ref.1, bf16[2048,256]{1,0:T(8,128)(2,1)} %k_ref.1, bf16[2048,256]{1,0:T(8,128)(2,1)} %v_ref.1, f32[3,7,2048]{2,1,0:T(8,128)} %taps_ref.1, bf16[256,2048]{1,0:T(8,128)(2,1)} %bitcast.1, f32[1,256]{1,0:T(1,128)} %gain_ref.1, ...), custom_call_target="tpu_custom_call" | custom-call | tf_op jit(solution)/shard_map/hyena/pallas_call | solution.py:361
  35.6 2.3 %copy.10 = bf16[2048,256]{1,0:T(8,128)(2,1)} copy(bf16[2048,256]{1,0:T(8,128)(2,1)} %hyena.1) | data formatting | bytes 2097152
where the time goes:
time: 38 us; the launch traced here: 37.8 us
  Pallas kernels  35.6 us (94%)
  local copies, waits for them, and re-layouts  2.26 us (6%)
    pallas_call x1, Pallas kernels, local(): pl.pallas_call(functools.partial(kernel, n, lanes), out_shape=jax.ShapeDt...  35.6 us
    unnamed x1, local copies, waits for them, and re-layouts  2.26 us

commit v1 on v0

--- a/solution.py
+++ b/solution.py
@@ -78,6 +78,382 @@
 
 def across(eye, block):
     return lax.dot_general(eye, block, (((1,), (1,)), ((), ())), preferred_element_type=F32)
+
+
+def crossed(a, b, count):
+    total, place = 0, 1
+    while place < count:
+        total = total + lax.rem(lax.div(a, place) + lax.div(b, place), 2) * place
+        place *= 2
+    return total
+
+
+def wide_kernel(
+    n,
+    q_hbm, k_hbm, v_hbm, taps_hbm, filt_hbm, gain_hbm, table_hbm, twist_hbm,
+    out_ref,
+    source, taps_ref, filt_ref, gain_ref, table_ref, twist_ref,
+    eye, tails, halo, turned, rim, gated, recv, spec, h_spec, ret, filt_rows, twist,
+    load_sem, q_sem, side_sem, halo_send, halo_recv,
+    rim_send, rim_recv, in_send, in_recv, in_own, out_send, out_recv, out_own,
+):
+    me = lax.axis_index("ctx")
+    width, tok = q_hbm.shape
+    chan, length = filt_hbm.shape
+    lanes = LANES
+    chunks = chan // lanes
+    reach = taps_hbm.shape[1]
+    blocks = length // LANES
+    tiles = tok // LANES
+    pairs = n // 2
+    step = 16
+    edge = 16
+    part = 64
+
+    barrier = pltpu.get_barrier_semaphore()
+    for d in range(1, n):
+        pl.semaphore_signal(
+            barrier, inc=1, device_id={"ctx": lax.rem(me + d, n)}, device_id_type=MESH
+        )
+
+    def peer_of(j):
+        return crossed(me, n - 1 - j, n)
+
+    def peer_rows(peer, c):
+        return pl.ds(pl.multiple_of(peer * chan + c * lanes, lanes), lanes)
+
+    def load(w, c, j):
+        ref = (q_hbm, k_hbm, v_hbm)[w]
+        at = peer_rows(peer_of(j), c)
+        return pltpu.make_async_copy(ref.at[at, :], source.at[w, at, :], load_sem.at[w - 1, c, j])
+
+    side = [
+        pltpu.make_async_copy(taps_hbm, taps_ref, side_sem.at[0]),
+        pltpu.make_async_copy(filt_hbm, filt_ref, side_sem.at[1]),
+        pltpu.make_async_copy(gain_hbm, gain_ref, side_sem.at[2]),
+        pltpu.make_async_copy(table_hbm, table_ref, side_sem.at[3]),
+        pltpu.make_async_copy(twist_hbm, twist_ref, side_sem.at[4]),
+    ]
+    load_q = pltpu.make_async_copy(q_hbm, source.at[0], q_sem)
+
+    def load_step(j, c):
+        load(1, c, j).start()
+        load(2, c, j).start()
+        return c
+
+    def load_wait(j, c):
+        load(1, c, j).wait()
+        load(2, c, j).wait()
+        return c
+
+    lax.fori_loop(0, 2, load_step, 0)
+    side[0].start()
+    lax.fori_loop(2, n, load_step, 0)
+    for c in range(1, chunks):
+        lax.fori_loop(0, n, load_step, c)
+    for i in range(1, len(side)):
+        side[i].start()
+    load_q.start()
+
+    size = eye.shape[0]
+    row = lax.broadcasted_iota(jnp.int32, (size, size), 0)
+    col = lax.broadcasted_iota(jnp.int32, (size, size), 1)
+    eye[...] = (row == col).astype(F32).astype(BF16)
+    pick_row = lax.broadcasted_iota(jnp.int32, (SLOT, LANES), 0) + (LANES - SLOT)
+    pick = (pick_row == lax.broadcasted_iota(jnp.int32, (SLOT, LANES), 1)).astype(F32).astype(BF16)
+
+    def find_tails(w):
+        def one(p, _):
+            at = pl.ds(pl.multiple_of(p * chan, chan), chan)
+            tails[w, p] = across(pick, source[w, at, tok - LANES :]).astype(BF16)
+            return 0
+
+        lax.fori_loop(0, n, one, 0, unroll=4)
+
+    def halo_copy(part_of):
+        at = slice(1, 3) if part_of == 0 else slice(0, 1)
+        return pltpu.make_async_remote_copy(
+            src_ref=tails.at[at], dst_ref=halo.at[at],
+            send_sem=halo_send.at[part_of], recv_sem=halo_recv.at[part_of],
+            device_id={"ctx": lax.rem(me + 1, n)}, device_id_type=MESH,
+        )
+
+    def halo_start(part_of):
+        @pl.when(me < n - 1)
+        def _():
+            halo_copy(part_of).start()
+
+    def halo_wait(part_of):
+        @pl.when(me < n - 1)
+        def _():
+            halo_copy(part_of).wait_send()
+
+        @pl.when(me > 0)
+        def _():
+            halo_copy(part_of).wait_recv()
+
+    def chunk_lanes(c):
+        return slice(c * lanes, (c + 1) * lanes)
+
+    def leaf_lanes(leaf):
+        return slice((leaf % 2) * LANES, (leaf % 2) * LANES + lanes)
+
+    def set_halo(w, peer, c, ref, *index):
+        ref[(*index, slice(0, SLOT), slice(None))] = jnp.zeros((SLOT, lanes), F32)
+
+        @pl.when(me > 0)
+        def _():
+            ref[(*index, slice(0, SLOT), slice(None))] = halo[w, peer, :, chunk_lanes(c)].astype(F32)
+
+    def turn_pair(first, pair, c, whole):
+        block = jnp.concatenate([source[w, peer_rows(peer, c), :] for w, peer in pair], axis=0)
+        both = across(eye[:tok, :tok], block)
+        for i, (w, peer) in enumerate(pair):
+            rows = both[:, i * lanes : (i + 1) * lanes]
+            turned[first + i, SLOT:, :] = rows
+            if whole:
+                set_halo(w, peer, c, turned, first + i)
+            else:
+                rim[w - 1, peer, SLOT:, :] = rows[:edge]
+        return [taps_ref[w, :, peer_rows(peer, c)] for w, peer in pair]
+
+    def sums_of(ref, index, taps, start, count):
+        total = None
+        for j in range(reach):
+            at = slice(SLOT - j + start, SLOT - j + start + count)
+            term = taps[j : j + 1, :] * ref[(*index, at, slice(None))]
+            total = term if total is None else total + term
+        return total
+
+    def spans(first):
+        marks = [first] + list(range((first // part + 1) * part, tok, part)) + [tok]
+        return list(zip(marks[:-1], marks[1:]))
+
+    def gate_pair(peers, c, whole):
+        taps = [turn_pair(2 * i, [(1, p), (2, p)], c, whole) for i, p in enumerate(peers)]
+        for i, p in enumerate(peers):
+            for start, stop in spans(0 if whole else edge):
+                count = stop - start
+                product = sums_of(turned, (2 * i,), taps[i][0], start, count) * sums_of(
+                    turned, (2 * i + 1,), taps[i][1], start, count
+                )
+                gated[c, p, start:stop, :] = product.astype(BF16)
+
+    def in_copy(c, j):
+        peer = peer_of(j)
+        at = slice(0 if c else edge, tok)
+        return pltpu.make_async_remote_copy(
+            src_ref=gated.at[c, peer, at, :], dst_ref=recv.at[c, me, at, :],
+            send_sem=in_send.at[c, j], recv_sem=in_recv.at[c, j],
+            device_id={"ctx": peer}, device_id_type=MESH,
+        )
+
+    def rim_copy(j):
+        peer = peer_of(j)
+        return pltpu.make_async_remote_copy(
+            src_ref=gated.at[0, peer, 0:edge, :], dst_ref=recv.at[0, me, 0:edge, :],
+            send_sem=rim_send.at[j], recv_sem=rim_recv.at[j],
+            device_id={"ctx": peer}, device_id_type=MESH,
+        )
+
+    def own_in(c):
+        return pltpu.make_async_copy(gated.at[c, me], recv.at[c, me], in_own.at[c])
+
+    def out_copy(c, j):
+        peer = peer_of(j)
+        return pltpu.make_async_remote_copy(
+            src_ref=recv.at[c, peer], dst_ref=ret.at[c, me],
+            send_sem=out_send.at[c, j], recv_sem=out_recv.at[c, j],
+            device_id={"ctx": peer}, device_id_type=MESH,
+        )
+
+    def own_out(c):
+        return pltpu.make_async_copy(recv.at[c, me], ret.at[c, me], out_own.at[c])
+
+    def gate_chunk(c):
+        def one(i, _):
+            if c == 0:
+                load_wait(2 * i, c)
+                load_wait(2 * i + 1, c)
+            gate_pair([peer_of(2 * i), peer_of(2 * i + 1)], c, c > 0)
+
+            @pl.when(i > 0)
+            def _():
+                in_copy(c, 2 * i - 2).start()
+                in_copy(c, 2 * i - 1).start()
+
+            return 0
+
+        if c == 0:
+            one_first(one)
+        else:
+            lax.fori_loop(0, pairs, one, 0)
+        in_copy(c, n - 2).start()
+
+    def one_first(one):
+        side[0].wait()
+        pl.semaphore_wait(barrier, n - 1)
+        lax.fori_loop(0, pairs, one, 0)
+
+    gate_chunk(0)
+    for c in range(1, chunks):
+        lax.fori_loop(0, n, load_wait, c)
+    find_tails(1)
+    find_tails(2)
+    halo_start(0)
+    halo_wait(0)
+
+    def rim_step(i, _):
+        for p in (peer_of(2 * i), peer_of(2 * i + 1)):
+            for w in (1, 2):
+                set_halo(w, p, 0, rim, w - 1, p)
+            gated[0, p, :edge, :] = (
+                sums_of(rim, (0, p), taps_ref[1, :, peer_rows(p, 0)], 0, edge)
+                * sums_of(rim, (1, p), taps_ref[2, :, peer_rows(p, 0)], 0, edge)
+            ).astype(BF16)
+        return 0
+
+    lax.fori_loop(0, pairs, rim_step, 0)
+
+    def rim_start(j, _):
+        rim_copy(j).start()
+        return 0
+
+    lax.fori_loop(0, n - 1, rim_start, 0)
+    own_in(0).start()
+
+    for c in range(1, chunks):
+        gate_chunk(c)
+        own_in(c).start()
+
+    load_q.wait()
+    find_tails(0)
+    halo_start(1)
+
+    for i in range(1, len(side)):
+        side[i].wait()
+    for a in range(blocks):
+        filt_rows[a // tiles, (a % tiles) * LANES : (a % tiles + 1) * LANES, :] = across(
+            eye[:LANES, :LANES], filt_ref[:, a * LANES : (a + 1) * LANES]
+        ).astype(BF16)
+
+    def short_stage(fetch_rows, first=False):
+        def one(r, _):
+            re_at = pl.ds(pl.multiple_of(r * step, step), step)
+            im_at = pl.ds(pl.multiple_of(LANES + r * step, step), step)
+
+            def emit(leaf, re, im):
+                if first:
+                    for which in range(2):
+                        column = twist_ref[re_at, which * blocks + leaf : which * blocks + leaf + 1]
+                        twist[leaf, which, re_at, :] = jnp.broadcast_to(column, (step, lanes))
+                cos, sin = twist[leaf, 0, re_at, :], twist[leaf, 1, re_at, :]
+                spec[leaf // 2, re_at, leaf_lanes(leaf)] = (re * cos - im * sin).astype(BF16)
+                spec[leaf // 2, im_at, leaf_lanes(leaf)] = (re * sin + im * cos).astype(BF16)
+
+            coefs = []
+            for a in range(blocks):
+                at = pl.ds(pl.multiple_of((a % tiles) * LANES + r * step, step), step)
+                x, lean = fetch_rows(a // tiles, at).astype(F32), a * math.pi / (2 * blocks)
+                coefs.append((x * math.cos(lean), x * math.sin(lean)))
+            split_forward(coefs, 0.0, 0, emit)
+            return 0
+
+        lax.fori_loop(0, LANES // step, one, 0)
+
+    def filter_chunk(c):
+        short_stage(lambda a, at: filt_rows[a, at, chunk_lanes(c)], c == 0)
+
+        def filt_pair(pair, _):
+            h_spec[c, pair] = jnp.dot(table_ref[0], spec[pair], preferred_element_type=F32).astype(h_spec.dtype)
+            return 0
+
+        lax.fori_loop(0, blocks // 2, filt_pair, 0, unroll=2)
+
+    for c in range(chunks):
+        filter_chunk(c)
+
+    def rim_wait(j, _):
+        rim_copy(j).wait()
+        return 0
+
+    for c in range(chunks):
+        def wait_in(j, _):
+            in_copy(c, j).wait()
+            return 0
+
+        lax.fori_loop(0, n - 1, wait_in, 0)
+        if c == 0:
+            lax.fori_loop(0, n - 1, rim_wait, 0)
+        own_in(c).wait()
+        short_stage(lambda a, at: recv[c, a, at, :])
+
+        def pair_step(pair, _):
+            sig = jnp.dot(table_ref[0], spec[pair], preferred_element_type=F32)
+            h_re, h_im = h_spec[c, pair, :LANES, :].astype(F32), h_spec[c, pair, LANES:, :].astype(F32)
+            s_re, s_im = sig[:LANES], sig[LANES:]
+            prod = jnp.concatenate([s_re * h_re - s_im * h_im, s_re * h_im + s_im * h_re], axis=0).astype(BF16)
+            h_spec[c, pair] = jnp.dot(table_ref[1], prod, preferred_element_type=F32).astype(h_spec.dtype)
+            return 0
+
+        lax.fori_loop(0, blocks // 2, pair_step, 0, unroll=4)
+        gain = gain_ref[:, chunk_lanes(c)]
+
+        def back_step(r, _):
+            re_at = pl.ds(pl.multiple_of(r * step, step), step)
+            im_at = pl.ds(pl.multiple_of(LANES + r * step, step), step)
+
+            def fetch(leaf):
+                re = h_spec[c, leaf // 2, re_at, leaf_lanes(leaf)].astype(F32)
+                im = h_spec[c, leaf // 2, im_at, leaf_lanes(leaf)].astype(F32)
+                cos, sin = twist[leaf, 0, re_at, :], twist[leaf, 1, re_at, :]
+                return re * cos + im * sin, im * cos - re * sin
+
+            parts = split_inverse(fetch, blocks, 0.0, 0)
+            for a, (re, im) in enumerate(parts):
+                lean = a * math.pi / (2 * blocks)
+                cos, sin = math.cos(lean) / length, math.sin(lean) / length
+                at = pl.ds(pl.multiple_of((a % tiles) * LANES + r * step, step), step)
+                sig = recv[c, a // tiles, at, :].astype(F32)
+                recv[c, a // tiles, at, :] = (cos * re + sin * im + gain * sig).astype(BF16)
+            return 0
+
+        lax.fori_loop(0, LANES // step, back_step, 0)
+
+        def return_step(j, _):
+            out_copy(c, j).start()
+            return 0
+
+        lax.fori_loop(0, n - 1, return_step, 0)
+        own_out(c).start()
+
+    halo_wait(1)
+    for c in range(chunks):
+        def q_step(i, _):
+            peers = (2 * i, 2 * i + 1)
+            taps = turn_pair(0, [(0, p) for p in peers], c, True)
+            for slot, p in enumerate(peers):
+                parts = [sums_of(turned, (slot,), taps[slot], start, part).astype(BF16) for start in range(0, tok, part)]
+                out_ref[peer_rows(p, c), :] = across(eye[:lanes, :lanes], jnp.concatenate(parts, axis=0)).astype(BF16)
+            return 0
+
+        lax.fori_loop(0, pairs, q_step, 0)
+
+    def mix(peer, c):
+        at = peer_rows(peer, c)
+        long = across(eye[:lanes, :lanes], ret[c, peer])
+        out_ref[at, :] = (out_ref[at, :].astype(F32) * long).astype(BF16)
+
+    for c in range(chunks):
+        own_out(c).wait()
+        mix(me, c)
+
+        def mix_step(j, _):
+            out_copy(c, j).wait()
+            mix(peer_of(j), c)
+            return 0
+
+        lax.fori_loop(0, n - 1, mix_step, 0)
 
 
 def kernel(
@@ -339,6 +715,65 @@
         lax.fori_loop(0, n, put_step, 0)
 
 
+def wide_call(n, queries, keys, values, taps, filters, gain):
+    width, tok = queries.shape
+    chan, length = filters.shape
+    blocks = length // LANES
+    chunks = chan // LANES
+    reach = taps.shape[1]
+    dma = pltpu.SemaphoreType.DMA
+    two = 2 * LANES
+    table = circle_tables()
+    columns = twist_columns(blocks)
+    held = [
+        pltpu.with_memory_space_constraint(x, pltpu.HBM)
+        for x in (queries, keys, values, taps, filters, gain, jnp.asarray(table), jnp.asarray(columns))
+    ]
+    return pl.pallas_call(
+        functools.partial(wide_kernel, n),
+        out_shape=pltpu.VMEM((width, tok), BF16),
+        in_specs=[pl.BlockSpec(memory_space=pltpu.HBM)] * 8,
+        out_specs=pl.BlockSpec(memory_space=pltpu.VMEM),
+        scratch_shapes=[
+            pltpu.VMEM((3, width, tok), BF16),
+            pltpu.VMEM((3, reach, width), F32),
+            pltpu.VMEM((chan, length), BF16),
+            pltpu.VMEM((1, chan), F32),
+            pltpu.VMEM(table.shape, BF16),
+            pltpu.VMEM(columns.shape, F32),
+            pltpu.VMEM((tok, tok), BF16),
+            pltpu.VMEM((3, n, SLOT, chan), BF16),
+            pltpu.VMEM((3, n, SLOT, chan), BF16),
+            pltpu.VMEM((4, SLOT + tok, LANES), F32),
+            pltpu.VMEM((2, n, SLOT + 16, LANES), F32),
+            pltpu.VMEM((chunks, n, tok, LANES), BF16),
+            pltpu.VMEM((chunks, n, tok, LANES), BF16),
+            pltpu.VMEM((blocks // 2, two, two), BF16),
+            pltpu.VMEM((chunks, blocks // 2, two, two), F32),
+            pltpu.VMEM((chunks, n, tok, LANES), BF16),
+            pltpu.VMEM((n, tok, chan), BF16),
+            pltpu.VMEM((blocks, 2, LANES, LANES), F32),
+            dma((2, chunks, n)),
+            dma,
+            dma((5,)),
+            dma((2,)),
+            dma((2,)),
+            dma((n,)),
+            dma((n,)),
+            dma((chunks, n)),
+            dma((chunks, n)),
+            dma((chunks,)),
+            dma((chunks, n)),
+            dma((chunks, n)),
+            dma((chunks,)),
+        ],
+        compiler_params=pltpu.CompilerParams(
+            collective_id=0, has_side_effects=True, vmem_limit_bytes=40 * 2**20
+        ),
+        name="hyena",
+    )(*held)
+
+
 def solution(mesh):
     n = mesh.shape["ctx"]
 
@@ -348,6 +783,9 @@
         blocks = length // LANES
         lanes = min(chan, LANES)
         chunks = chan // lanes
+        small_work = length * chan <= 2**20
+        if n >= 2 and n & (n - 1) == 0 and chan % LANES == 0 and tok % LANES == 0 and small_work:
+            return wide_call(n, queries, keys, values, short_taps, long_filter[0], skip_gain)
         table = jnp.asarray(circle_tables())
         twist = jnp.asarray(twist_columns(blocks))
         dma = pltpu.SemaphoreType.DMA

time: 38 us -> 39.1 us (1.029)
  Pallas kernels: 35.6 us -> 38 us
  local copies, waits for them, and re-layouts: 2.26 us -> 0.97 us
    pallas_call x1, Pallas kernels: 35.6 us -> 38 us  [wide_call(): pl.pallas_call(functools.partial(wide_kernel, n), out_shape=pltpu.VMEM((w...]
    unnamed x1, local copies, waits for them, and re-layouts: 2.26 us -> 0.97 us
where the time goes in v1:
time: 39.1 us; the launch traced here: 39 us
  Pallas kernels  38 us (97%)
  local copies, waits for them, and re-layouts  0.97 us (2%)
    pallas_call x1, Pallas kernels, wide_call(): pl.pallas_call(functools.partial(wide_kernel, n), out_shape=pltpu.VMEM((w...  38 us
    unnamed x1, local copies, waits for them, and re-layouts  0.97 us

profile of v1, /device:TPU:0, one launch (start us, length us, event | category | flops | bytes accessed | tf_op | source)
XLA Modules:
  0.0 39.0 jit_solution(878228112329223229)
XLA Ops:
  0.0 38.0 %hyena.1 = bf16[2048,256]{1,0:T(8,128)(2,1)S(1)} custom-call(bf16[2048,256]{1,0:T(8,128)(2,1)} %q_hbm.1, bf16[2048,256]{1,0:T(8,128)(2,1)} %k_hbm.1, bf16[2048,256]{1,0:T(8,128)(2,1)} %v_hbm.1, f32[3,7,2048]{2,1,0:T(8,128)} %taps_hbm.1, bf16[256,2048]{1,0:T(8,128)(2,1)} %bitcast.1, f32[1,256]{1,0:T(1,128)} %gain_hbm.1, ...), custom_call_target="tpu_custom_call" | custom-call | tf_op jit(solution)/shard_map/hyena/pallas_call | solution.py:732
  38.0 1.0 %copy.10 = bf16[2048,256]{1,0:T(8,128)(2,1)} copy(bf16[2048,256]{1,0:T(8,128)(2,1)S(1)} %hyena.1) | data formatting | bytes 2097152

commit v2 on v1

--- a/solution.py
+++ b/solution.py
@@ -80,6 +80,13 @@
     return lax.dot_general(eye, block, (((1,), (1,)), ((), ())), preferred_element_type=F32)
 
 
+def wave_tables(tok):
+    bins = np.concatenate([np.arange(0, tok, 2), np.arange(1, tok, 2)])
+    angle = (2 * bins + 1)[:, None] * np.arange(tok)[None, :] * (math.pi / (2 * tok))
+    there = np.concatenate([np.cos(angle), np.sin(angle)], axis=0)
+    return there.astype(ml_dtypes.bfloat16), (there.T / tok).astype(ml_dtypes.bfloat16)
+
+
 def crossed(a, b, count):
     total, place = 0, 1
     while place < count:
@@ -90,10 +97,10 @@
 
 def wide_kernel(
     n,
-    q_hbm, k_hbm, v_hbm, taps_hbm, filt_hbm, gain_hbm, table_hbm, twist_hbm,
+    q_hbm, k_hbm, v_hbm, taps_hbm, filt_hbm, gain_hbm, there_hbm, back_hbm,
     out_ref,
-    source, taps_ref, filt_ref, gain_ref, table_ref, twist_ref,
-    eye, tails, halo, turned, rim, gated, recv, spec, h_spec, ret, filt_rows, twist,
+    source, taps_ref, filt_ref, gain_ref, there_ref, back_ref,
+    eye, tails, halo, turned, rim, gated, recv, ret, q_rows, wave, filt_wave, sig_wave, out_wave,
     load_sem, q_sem, side_sem, halo_send, halo_recv,
     rim_send, rim_recv, in_send, in_recv, in_own, out_send, out_recv, out_own,
 ):
@@ -103,10 +110,9 @@
     lanes = LANES
     chunks = chan // lanes
     reach = taps_hbm.shape[1]
-    blocks = length // LANES
-    tiles = tok // LANES
     pairs = n // 2
     step = 16
+    half = step // 2
     edge = 16
     part = 64
 
@@ -131,8 +137,8 @@
         pltpu.make_async_copy(taps_hbm, taps_ref, side_sem.at[0]),
         pltpu.make_async_copy(filt_hbm, filt_ref, side_sem.at[1]),
         pltpu.make_async_copy(gain_hbm, gain_ref, side_sem.at[2]),
-        pltpu.make_async_copy(table_hbm, table_ref, side_sem.at[3]),
-        pltpu.make_async_copy(twist_hbm, twist_ref, side_sem.at[4]),
+        pltpu.make_async_copy(there_hbm, there_ref, side_sem.at[3]),
+        pltpu.make_async_copy(back_hbm, back_ref, side_sem.at[4]),
     ]
     load_q = pltpu.make_async_copy(q_hbm, source.at[0], q_sem)
 
@@ -194,9 +200,6 @@
 
     def chunk_lanes(c):
         return slice(c * lanes, (c + 1) * lanes)
-
-    def leaf_lanes(leaf):
-        return slice((leaf % 2) * LANES, (leaf % 2) * LANES + lanes)
 
     def set_halo(w, peer, c, ref, *index):
         ref[(*index, slice(0, SLOT), slice(None))] = jnp.zeros((SLOT, lanes), F32)
@@ -301,6 +304,33 @@
     find_tails(1)
     find_tails(2)
     halo_start(0)
+
+    for i in range(1, len(side)):
+        side[i].wait()
+
+    mid = tok // 2
+    signs = ((0, 1.0), (mid, -1.0))
+
+    def filter_wave(d):
+        wave[d % 2] = across(there_ref[...], filt_ref[:, d * tok : (d + 1) * tok])
+        now, before = wave.at[d % 2], wave.at[1 - d % 2]
+
+        def one(r, _):
+            for first, sign in signs:
+                re_at = pl.ds(pl.multiple_of(first + r * step, step), step)
+                im_at = pl.ds(pl.multiple_of(tok + first + r * step, step), step)
+                re, im = now[re_at, :], now[im_at, :]
+                if d > 0:
+                    re, im = re + sign * before[im_at, :], im - sign * before[re_at, :]
+                for c in range(chunks):
+                    filt_wave[c, d, re_at, :] = re[:, chunk_lanes(c)]
+                    filt_wave[c, d, im_at, :] = im[:, chunk_lanes(c)]
+            return 0
+
+        lax.fori_loop(0, mid // step, one, 0, unroll=2)
+
+    for d in range(n):
+        filter_wave(d)
     halo_wait(0)
 
     def rim_step(i, _):
@@ -330,127 +360,116 @@
     find_tails(0)
     halo_start(1)
 
-    for i in range(1, len(side)):
-        side[i].wait()
-    for a in range(blocks):
-        filt_rows[a // tiles, (a % tiles) * LANES : (a % tiles + 1) * LANES, :] = across(
-            eye[:LANES, :LANES], filt_ref[:, a * LANES : (a + 1) * LANES]
-        ).astype(BF16)
-
-    def short_stage(fetch_rows, first=False):
+    def sig_step(c):
+        def one(i, _):
+            in_copy(c, 2 * i).wait()
+            if c == 0:
+                rim_copy(2 * i).wait()
+
+            @pl.when(i < pairs - 1)
+            def _():
+                in_copy(c, 2 * i + 1).wait()
+                if c == 0:
+                    rim_copy(2 * i + 1).wait()
+
+            @pl.when(i == pairs - 1)
+            def _():
+                own_in(c).wait()
+
+            first = lax.div(peer_of(2 * i), 2) * 2
+            both = jnp.concatenate([recv[c, first], recv[c, first + 1]], axis=1)
+            both = jnp.dot(there_ref[...], both, preferred_element_type=F32)
+            sig_wave[first] = both[:, :lanes]
+            sig_wave[first + 1] = both[:, lanes:]
+            return 0
+
+        lax.fori_loop(0, pairs, one, 0)
+
+    def blend(c):
         def one(r, _):
+            done = []
+            for part_of in range(2):
+                start = r * step + part_of * half
+                re_at = pl.ds(pl.multiple_of(start, half), half)
+                im_at = pl.ds(pl.multiple_of(tok + start, half), half)
+                f_re = [filt_wave[c, d, re_at, :] for d in range(n)]
+                f_im = [filt_wave[c, d, im_at, :] for d in range(n)]
+                s_re = [sig_wave[d, re_at, :] for d in range(n)]
+                s_im = [sig_wave[d, im_at, :] for d in range(n)]
+                rows = []
+                for i in range(n):
+                    re = im = None
+                    for j in range(i + 1):
+                        a, b, x, y = f_re[i - j], f_im[i - j], s_re[j], s_im[j]
+                        re = a * x - b * y if re is None else re + a * x - b * y
+                        im = a * y + b * x if im is None else im + a * y + b * x
+                    rows.append((re, im))
+                done.append(rows)
             re_at = pl.ds(pl.multiple_of(r * step, step), step)
-            im_at = pl.ds(pl.multiple_of(LANES + r * step, step), step)
-
-            def emit(leaf, re, im):
-                if first:
-                    for which in range(2):
-                        column = twist_ref[re_at, which * blocks + leaf : which * blocks + leaf + 1]
-                        twist[leaf, which, re_at, :] = jnp.broadcast_to(column, (step, lanes))
-                cos, sin = twist[leaf, 0, re_at, :], twist[leaf, 1, re_at, :]
-                spec[leaf // 2, re_at, leaf_lanes(leaf)] = (re * cos - im * sin).astype(BF16)
-                spec[leaf // 2, im_at, leaf_lanes(leaf)] = (re * sin + im * cos).astype(BF16)
-
-            coefs = []
-            for a in range(blocks):
-                at = pl.ds(pl.multiple_of((a % tiles) * LANES + r * step, step), step)
-                x, lean = fetch_rows(a // tiles, at).astype(F32), a * math.pi / (2 * blocks)
-                coefs.append((x * math.cos(lean), x * math.sin(lean)))
-            split_forward(coefs, 0.0, 0, emit)
-            return 0
-
-        lax.fori_loop(0, LANES // step, one, 0)
-
-    def filter_chunk(c):
-        short_stage(lambda a, at: filt_rows[a, at, chunk_lanes(c)], c == 0)
-
-        def filt_pair(pair, _):
-            h_spec[c, pair] = jnp.dot(table_ref[0], spec[pair], preferred_element_type=F32).astype(h_spec.dtype)
-            return 0
-
-        lax.fori_loop(0, blocks // 2, filt_pair, 0, unroll=2)
-
-    for c in range(chunks):
-        filter_chunk(c)
-
-    def rim_wait(j, _):
-        rim_copy(j).wait()
-        return 0
-
-    for c in range(chunks):
-        def wait_in(j, _):
-            in_copy(c, j).wait()
-            return 0
-
-        lax.fori_loop(0, n - 1, wait_in, 0)
-        if c == 0:
-            lax.fori_loop(0, n - 1, rim_wait, 0)
-        own_in(c).wait()
-        short_stage(lambda a, at: recv[c, a, at, :])
-
-        def pair_step(pair, _):
-            sig = jnp.dot(table_ref[0], spec[pair], preferred_element_type=F32)
-            h_re, h_im = h_spec[c, pair, :LANES, :].astype(F32), h_spec[c, pair, LANES:, :].astype(F32)
-            s_re, s_im = sig[:LANES], sig[LANES:]
-            prod = jnp.concatenate([s_re * h_re - s_im * h_im, s_re * h_im + s_im * h_re], axis=0).astype(BF16)
-            h_spec[c, pair] = jnp.dot(table_ref[1], prod, preferred_element_type=F32).astype(h_spec.dtype)
-            return 0
-
-        lax.fori_loop(0, blocks // 2, pair_step, 0, unroll=4)
+            im_at = pl.ds(pl.multiple_of(tok + r * step, step), step)
+            for i in range(n):
+                at = slice((i % 2) * lanes, (i % 2 + 1) * lanes)
+                for which, rows_at in enumerate((re_at, im_at)):
+                    whole = jnp.concatenate([done[0][i][which], done[1][i][which]], axis=0)
+                    out_wave[i // 2, rows_at, at] = whole.astype(BF16)
+            return 0
+
+        lax.fori_loop(0, tok // step, one, 0)
+
+    def return_step(c):
         gain = gain_ref[:, chunk_lanes(c)]
 
-        def back_step(r, _):
-            re_at = pl.ds(pl.multiple_of(r * step, step), step)
-            im_at = pl.ds(pl.multiple_of(LANES + r * step, step), step)
-
-            def fetch(leaf):
-                re = h_spec[c, leaf // 2, re_at, leaf_lanes(leaf)].astype(F32)
-                im = h_spec[c, leaf // 2, im_at, leaf_lanes(leaf)].astype(F32)
-                cos, sin = twist[leaf, 0, re_at, :], twist[leaf, 1, re_at, :]
-                return re * cos + im * sin, im * cos - re * sin
-
-            parts = split_inverse(fetch, blocks, 0.0, 0)
-            for a, (re, im) in enumerate(parts):
-                lean = a * math.pi / (2 * blocks)
-                cos, sin = math.cos(lean) / length, math.sin(lean) / length
-                at = pl.ds(pl.multiple_of((a % tiles) * LANES + r * step, step), step)
-                sig = recv[c, a // tiles, at, :].astype(F32)
-                recv[c, a // tiles, at, :] = (cos * re + sin * im + gain * sig).astype(BF16)
-            return 0
-
-        lax.fori_loop(0, LANES // step, back_step, 0)
-
-        def return_step(j, _):
-            out_copy(c, j).start()
-            return 0
-
-        lax.fori_loop(0, n - 1, return_step, 0)
+        def one(i, _):
+            couple = lax.div(peer_of(2 * i), 2)
+            both = jnp.dot(back_ref[...], out_wave[couple], preferred_element_type=F32)
+            for k in range(2):
+                sig = recv[c, 2 * couple + k].astype(F32)
+                recv[c, 2 * couple + k] = (both[:, k * lanes : (k + 1) * lanes] + gain * sig).astype(BF16)
+
+            @pl.when(i > 0)
+            def _():
+                out_copy(c, 2 * i - 2).start()
+                out_copy(c, 2 * i - 1).start()
+
+            return 0
+
+        lax.fori_loop(0, pairs, one, 0)
+        out_copy(c, n - 2).start()
         own_out(c).start()
 
-    halo_wait(1)
-    for c in range(chunks):
-        def q_step(i, _):
+    def q_chunk(c):
+        def one(i, _):
             peers = (2 * i, 2 * i + 1)
             taps = turn_pair(0, [(0, p) for p in peers], c, True)
             for slot, p in enumerate(peers):
-                parts = [sums_of(turned, (slot,), taps[slot], start, part).astype(BF16) for start in range(0, tok, part)]
-                out_ref[peer_rows(p, c), :] = across(eye[:lanes, :lanes], jnp.concatenate(parts, axis=0)).astype(BF16)
-            return 0
-
-        lax.fori_loop(0, pairs, q_step, 0)
+                for start in range(0, tok, part):
+                    q_rows[c, p, start : start + part, :] = sums_of(
+                        turned, (slot,), taps[slot], start, part
+                    ).astype(BF16)
+            return 0
+
+        lax.fori_loop(0, pairs, one, 0)
+
+    for c in range(chunks):
+        sig_step(c)
+        blend(c)
+        return_step(c)
+        if c == 0:
+            halo_wait(1)
+        q_chunk(c)
 
     def mix(peer, c):
-        at = peer_rows(peer, c)
-        long = across(eye[:lanes, :lanes], ret[c, peer])
-        out_ref[at, :] = (out_ref[at, :].astype(F32) * long).astype(BF16)
+        long = ret[c, peer].astype(F32)
+        mixed = (q_rows[c, peer].astype(F32) * long).astype(BF16)
+        out_ref[peer_rows(peer, c), :] = across(eye[:lanes, :lanes], mixed).astype(BF16)
 
     for c in range(chunks):
         own_out(c).wait()
         mix(me, c)
 
         def mix_step(j, _):
-            out_copy(c, j).wait()
-            mix(peer_of(j), c)
+            out_copy(c, n - 2 - j).wait()
+            mix(peer_of(n - 2 - j), c)
             return 0
 
         lax.fori_loop(0, n - 1, mix_step, 0)
@@ -718,16 +737,13 @@
 def wide_call(n, queries, keys, values, taps, filters, gain):
     width, tok = queries.shape
     chan, length = filters.shape
-    blocks = length // LANES
     chunks = chan // LANES
     reach = taps.shape[1]
     dma = pltpu.SemaphoreType.DMA
-    two = 2 * LANES
-    table = circle_tables()
-    columns = twist_columns(blocks)
+    there, back = wave_tables(tok)
     held = [
         pltpu.with_memory_space_constraint(x, pltpu.HBM)
-        for x in (queries, keys, values, taps, filters, gain, jnp.asarray(table), jnp.asarray(columns))
+        for x in (queries, keys, values, taps, filters, gain, jnp.asarray(there), jnp.asarray(back))
     ]
     return pl.pallas_call(
         functools.partial(wide_kernel, n),
@@ -739,8 +755,8 @@
             pltpu.VMEM((3, reach, width), F32),
             pltpu.VMEM((chan, length), BF16),
             pltpu.VMEM((1, chan), F32),
-            pltpu.VMEM(table.shape, BF16),
-            pltpu.VMEM(columns.shape, F32),
+            pltpu.VMEM(there.shape, BF16),
+            pltpu.VMEM(back.shape, BF16),
             pltpu.VMEM((tok, tok), BF16),
             pltpu.VMEM((3, n, SLOT, chan), BF16),
             pltpu.VMEM((3, n, SLOT, chan), BF16),
@@ -748,11 +764,12 @@
             pltpu.VMEM((2, n, SLOT + 16, LANES), F32),
             pltpu.VMEM((chunks, n, tok, LANES), BF16),
             pltpu.VMEM((chunks, n, tok, LANES), BF16),
-            pltpu.VMEM((blocks // 2, two, two), BF16),
-            pltpu.VMEM((chunks, blocks // 2, two, two), F32),
             pltpu.VMEM((chunks, n, tok, LANES), BF16),
-            pltpu.VMEM((n, tok, chan), BF16),
-            pltpu.VMEM((blocks, 2, LANES, LANES), F32),
+            pltpu.VMEM((chunks, n, tok, LANES), BF16),
+            pltpu.VMEM((2, 2 * tok, chan), F32),
+            pltpu.VMEM((chunks, n, 2 * tok, LANES), F32),
+            pltpu.VMEM((n, 2 * tok, LANES), F32),
+            pltpu.VMEM((n // 2, 2 * tok, 2 * LANES), BF16),
             dma((2, chunks, n)),
             dma,
             dma((5,)),
@@ -784,7 +801,7 @@
         lanes = min(chan, LANES)
         chunks = chan // lanes
         small_work = length * chan <= 2**20
-        if n >= 2 and n & (n - 1) == 0 and chan % LANES == 0 and tok % LANES == 0 and small_work:
+        if n >= 2 and n & (n - 1) == 0 and chan % LANES == 0 and tok % LANES == 0 and length == n * tok and small_work:
             return wide_call(n, queries, keys, values, short_taps, long_filter[0], skip_gain)
         table = jnp.asarray(circle_tables())
         twist = jnp.asarray(twist_columns(blocks))

time: 39.1 us -> 35.8 us (0.916)
  Pallas kernels: 38 us -> 34.6 us
    pallas_call x1, Pallas kernels: 38 us -> 34.6 us  [wide_call(): pl.pallas_call(functools.partial(wide_kernel, n), out_shape=pltpu.VMEM((w...]
where the time goes in v2:
time: 35.8 us; the launch traced here: 35.6 us
  Pallas kernels  34.6 us (97%)
  local copies, waits for them, and re-layouts  0.97 us (3%)
    pallas_call x1, Pallas kernels, wide_call(): pl.pallas_call(functools.partial(wide_kernel, n), out_shape=pltpu.VMEM((w...  34.6 us
    unnamed x1, local copies, waits for them, and re-layouts  0.97 us

profile of v2, /device:TPU:0, one launch (start us, length us, event | category | flops | bytes accessed | tf_op | source)
XLA Modules:
  0.0 35.6 jit_solution(2118275152859991643)
XLA Ops:
  0.0 34.6 %hyena.1 = bf16[2048,256]{1,0:T(8,128)(2,1)S(1)} custom-call(bf16[2048,256]{1,0:T(8,128)(2,1)} %q_hbm.1, bf16[2048,256]{1,0:T(8,128)(2,1)} %k_hbm.1, bf16[2048,256]{1,0:T(8,128)(2,1)} %v_hbm.1, f32[3,7,2048]{2,1,0:T(8,128)} %taps_hbm.1, bf16[256,2048]{1,0:T(8,128)(2,1)} %bitcast.1, f32[1,256]{1,0:T(1,128)} %gain_hbm.1, ...), custom_call_target="tpu_custom_call" | custom-call | tf_op jit(solution)/shard_map/hyena/pallas_call | solution.py:748
  34.6 1.0 %copy.10 = bf16[2048,256]{1,0:T(8,128)(2,1)} copy(bf16[2048,256]{1,0:T(8,128)(2,1)S(1)} %hyena.1) | data formatting | bytes 2097152

commit v3 on v0

--- a/solution.py
+++ b/solution.py
@@ -78,6 +78,426 @@
 
 def across(eye, block):
     return lax.dot_general(eye, block, (((1,), (1,)), ((), ())), preferred_element_type=F32)
+
+
+def crossed(a, b, count):
+    total, place = 0, 1
+    while place < count:
+        total = total + lax.rem(lax.div(a, place) + lax.div(b, place), 2) * place
+        place *= 2
+    return total
+
+
+def wave_tables(tok):
+    bins = np.concatenate([np.arange(0, tok, 2), np.arange(1, tok, 2)])
+    angle = (2 * bins + 1)[:, None] * np.arange(tok)[None, :] * (math.pi / (2 * tok))
+    there = np.concatenate([np.cos(angle), np.sin(angle)], axis=0)
+    return there.astype(ml_dtypes.bfloat16), (there.T / tok).astype(ml_dtypes.bfloat16)
+
+
+def send_order(n):
+    pairs = [(m, m - 1) for m in range(n - 1, 0, -2)]
+    return [(4, 2), (5, 3), (6, 7), (1, 0)] if n == 8 else pairs
+
+
+def wide_kernel(
+    n,
+    q_hbm, k_hbm, v_hbm, taps_hbm, filt_hbm, gain_hbm, there_hbm, back_hbm,
+    out_ref,
+    q_ref, source, taps_ref, filt_ref, gain_ref, there_ref, back_ref,
+    eye, tails, halo, q_tails, q_halo, turned_a, turned_b, rim, gated, recv, ret, q_rows,
+    wave, filt_wave, sig_wave, out_wave,
+    load_sem, rest_sem, q_sem, side_sem, halo_send, halo_recv,
+    rim_recv, in_send, in_recv, in_own, out_send, out_recv,
+):
+    me = lax.axis_index("ctx")
+    chunks, lanes, tok = q_hbm.shape[1:]
+    reach = taps_hbm.shape[1]
+    pairs = n // 2
+    step = 16
+    half = step // 2
+    edge = 16
+    part = 64
+    order = send_order(n)
+    first_code = sum(a * n**i for i, (a, _) in enumerate(order))
+    second_code = sum(b * n**i for i, (_, b) in enumerate(order))
+
+    barrier = pltpu.get_barrier_semaphore()
+    for d in range(1, n):
+        pl.semaphore_signal(
+            barrier, inc=1, device_id={"ctx": lax.rem(me + d, n)}, device_id_type=MESH
+        )
+
+    def met(m):
+        return crossed(me, m, n)
+
+    def load_start(m):
+        p = met(m)
+        for w, ref in enumerate((k_hbm, v_hbm)):
+            pltpu.make_async_copy(ref.at[p, 0], source.at[0, p, w], load_sem.at[m]).start()
+
+    def load_wait(m):
+        p = met(m)
+        pltpu.make_async_copy(source.at[0, p], source.at[0, p], load_sem.at[m]).wait()
+
+    def rest(c):
+        return [
+            pltpu.make_async_copy(ref.at[:, c], source.at[c, :, w], rest_sem.at[c, w])
+            for w, ref in enumerate((k_hbm, v_hbm))
+        ]
+
+    side = [
+        pltpu.make_async_copy(taps_hbm, taps_ref, side_sem.at[0]),
+        pltpu.make_async_copy(filt_hbm, filt_ref, side_sem.at[1]),
+        pltpu.make_async_copy(gain_hbm, gain_ref, side_sem.at[2]),
+        pltpu.make_async_copy(there_hbm, there_ref, side_sem.at[3]),
+        pltpu.make_async_copy(back_hbm, back_ref, side_sem.at[4]),
+    ]
+    load_q = pltpu.make_async_copy(q_hbm, q_ref, q_sem)
+
+    for i, (a, b) in enumerate(order):
+        load_start(jnp.int32(a))
+        load_start(jnp.int32(b))
+        if i == 0:
+            side[0].start()
+    for c in range(1, chunks):
+        for copy in rest(c):
+            copy.start()
+    for i in (1, 3, 2, 4):
+        side[i].start()
+    load_q.start()
+
+    size = eye.shape[0]
+    row = lax.broadcasted_iota(jnp.int32, (size, size), 0)
+    col = lax.broadcasted_iota(jnp.int32, (size, size), 1)
+    eye[...] = (row == col).astype(F32).astype(BF16)
+    pick_row = lax.broadcasted_iota(jnp.int32, (SLOT, LANES), 0) + (LANES - SLOT)
+    pick = (pick_row == lax.broadcasted_iota(jnp.int32, (SLOT, LANES), 1)).astype(F32).astype(BF16)
+
+    def peer_rows(peer, c):
+        return pl.ds(pl.multiple_of((peer * chunks + c) * lanes, lanes), lanes)
+
+    def chunk_lanes(c):
+        return slice(c * lanes, (c + 1) * lanes)
+
+    @pl.when(me == 0)
+    def _():
+        halo[...] = jnp.zeros_like(halo)
+        q_halo[...] = jnp.zeros_like(q_halo)
+
+    def halo_copy(which):
+        mine, theirs = ((tails, halo), (q_tails, q_halo))[which]
+        return pltpu.make_async_remote_copy(
+            src_ref=mine, dst_ref=theirs, send_sem=halo_send.at[which], recv_sem=halo_recv.at[which],
+            device_id={"ctx": lax.rem(me + 1, n)}, device_id_type=MESH,
+        )
+
+    def halo_start(which):
+        @pl.when(me < n - 1)
+        def _():
+            halo_copy(which).start()
+
+    def halo_wait(which):
+        @pl.when(me < n - 1)
+        def _():
+            halo_copy(which).wait_send()
+
+        @pl.when(me > 0)
+        def _():
+            halo_copy(which).wait_recv()
+
+    def find_tails():
+        for c in range(chunks):
+            def one(p, _):
+                block = source[c, p].reshape(2 * lanes, tok)
+                tails[c, p] = across(pick, block[:, tok - LANES :]).astype(BF16)
+                return 0
+
+            lax.fori_loop(0, n, one, 0, unroll=4)
+
+    def find_q_tails():
+        def one(p, _):
+            block = q_ref[p].reshape(chunks * lanes, tok)
+            q_tails[p] = across(pick, block[:, tok - LANES :]).astype(BF16)
+            return 0
+
+        lax.fori_loop(0, n, one, 0, unroll=4)
+
+    def turn(c, m, turned):
+        p = met(m)
+        both = across(eye[:tok, :tok], source[c, p].reshape(2 * lanes, tok))
+        for w in range(2):
+            rows = both[:, w * lanes : (w + 1) * lanes]
+            turned[w, SLOT:, :] = rows
+            if c > 0:
+                turned[w, :SLOT, :] = halo[c, p, :, w * lanes : (w + 1) * lanes].astype(F32)
+            else:
+                rim[w, p, SLOT:, :] = rows[:edge]
+
+    def sums_of(ref, index, taps, start, count):
+        total = None
+        for j in range(reach):
+            at = slice(SLOT - j + start, SLOT - j + start + count)
+            term = taps[j : j + 1, :] * ref[(*index, at, slice(None))]
+            total = term if total is None else total + term
+        return total
+
+    def spans(first):
+        marks = [first] + list(range((first // part + 1) * part, tok, part)) + [tok]
+        return list(zip(marks[:-1], marks[1:]))
+
+    def gate(c, m, turned):
+        p = met(m)
+        k_taps, v_taps = (taps_ref[w, :, peer_rows(p, c)] for w in (1, 2))
+        for start, stop in spans(0 if c else edge):
+            count = stop - start
+            product = sums_of(turned, (0,), k_taps, start, count) * sums_of(turned, (1,), v_taps, start, count)
+            gated[c, p, start:stop, :] = product.astype(BF16)
+
+    def in_start(c, m):
+        peer = met(m)
+        at = slice(0 if c else edge, tok)
+        pltpu.make_async_remote_copy(
+            src_ref=gated.at[c, peer, at, :], dst_ref=recv.at[c, me, at, :],
+            send_sem=in_send, recv_sem=in_recv.at[c, lax.div(m, 2)],
+            device_id={"ctx": peer}, device_id_type=MESH,
+        ).start()
+
+    def rim_start(m):
+        peer = met(m)
+        pltpu.make_async_remote_copy(
+            src_ref=gated.at[0, peer, 0:edge, :], dst_ref=recv.at[0, me, 0:edge, :],
+            send_sem=in_send, recv_sem=rim_recv,
+            device_id={"ctx": peer}, device_id_type=MESH,
+        ).start()
+
+    def own_in(c):
+        return pltpu.make_async_copy(gated.at[c, me], recv.at[c, me], in_own.at[c])
+
+    def out_copy(c, m):
+        peer = met(m)
+        return pltpu.make_async_remote_copy(
+            src_ref=recv.at[c, peer], dst_ref=ret.at[c, me],
+            send_sem=out_send, recv_sem=out_recv.at[c, m],
+            device_id={"ctx": peer}, device_id_type=MESH,
+        )
+
+    def await_bytes(ref, sem):
+        pltpu.make_async_copy(ref, ref, sem).wait()
+
+    def gate_chunk(c):
+        if c == 0:
+            for m in (*order[0], order[1][0]):
+                load_wait(jnp.int32(m))
+            side[0].wait()
+        turn(c, jnp.int32(order[0][0]), turned_a)
+        if c == 0:
+            pl.semaphore_wait(barrier, n - 1)
+
+        def one(i, codes):
+            a, b = lax.rem(codes[0], n), lax.rem(codes[1], n)
+            codes = (lax.div(codes[0], n), lax.div(codes[1], n))
+            after = lax.rem(codes[0], n)
+            if c == 0:
+                @pl.when(i == 1)
+                def _():
+                    for m in (order[1][1], *(m for pair in order[2:] for m in pair)):
+                        load_wait(jnp.int32(m))
+                    for k in range(1, chunks):
+                        for copy in rest(k):
+                            copy.wait()
+                    find_tails()
+                    halo_start(0)
+
+            turn(c, b, turned_b)
+            gate(c, a, turned_a)
+            in_start(c, a)
+            turn(c, after, turned_a)
+            gate(c, b, turned_b)
+
+            @pl.when(i < pairs - 1)
+            def _():
+                in_start(c, b)
+
+            return codes
+
+        lax.fori_loop(0, pairs, one, (jnp.int32(first_code), jnp.int32(second_code)))
+
+    def filter_wave(d):
+        wave[d % 2] = across(there_ref[...], filt_ref[:, d * tok : (d + 1) * tok])
+        now, before = wave.at[d % 2], wave.at[1 - d % 2]
+
+        def one(r, _):
+            for first, sign in ((0, 1.0), (tok // 2, -1.0)):
+                re_at = pl.ds(pl.multiple_of(first + r * step, step), step)
+                im_at = pl.ds(pl.multiple_of(tok + first + r * step, step), step)
+                re, im = now[re_at, :], now[im_at, :]
+                if d > 0:
+                    re, im = re + sign * before[im_at, :], im - sign * before[re_at, :]
+                for c in range(chunks):
+                    filt_wave[c, d, re_at, :] = re[:, chunk_lanes(c)]
+                    filt_wave[c, d, im_at, :] = im[:, chunk_lanes(c)]
+            return 0
+
+        lax.fori_loop(0, tok // 2 // step, one, 0, unroll=2)
+
+    def rim_step(p, _):
+        sums = []
+        for w in range(2):
+            rim[w, p, :SLOT, :] = halo[0, p, :, w * lanes : (w + 1) * lanes].astype(F32)
+            sums.append(sums_of(rim, (w, p), taps_ref[1 + w, :, peer_rows(p, 0)], 0, edge))
+        gated[0, p, :edge, :] = (sums[0] * sums[1]).astype(BF16)
+        return 0
+
+    def sig_couple(c, first):
+        both = jnp.concatenate([recv[c, first], recv[c, first + 1]], axis=1)
+        both = jnp.dot(there_ref[...], both, preferred_element_type=F32)
+        sig_wave[first] = both[:, :lanes]
+        sig_wave[first + 1] = both[:, lanes:]
+
+    def sig_chunk(c):
+        at = slice(0 if c else edge, tok)
+        if c == 0:
+            await_bytes(recv.at[0, 0 : n - 1, 0:edge, :], rim_recv)
+        own_in(c).wait()
+        await_bytes(recv.at[c, met(jnp.int32(1)), at, :], in_recv.at[c, 0])
+        sig_couple(c, 2 * lax.div(me, 2))
+
+        def one(x, _):
+            first = 2 * lax.div(met(2 * x), 2)
+            await_bytes(recv.at[c, pl.ds(first, 2), at, :], in_recv.at[c, x])
+            sig_couple(c, first)
+            return 0
+
+        lax.fori_loop(1, pairs, one, 0)
+
+    def blend(c):
+        def one(r, _):
+            done = []
+            for part_of in range(2):
+                start = r * step + part_of * half
+                re_at = pl.ds(pl.multiple_of(start, half), half)
+                im_at = pl.ds(pl.multiple_of(tok + start, half), half)
+                f_re = [filt_wave[c, d, re_at, :] for d in range(n)]
+                f_im = [filt_wave[c, d, im_at, :] for d in range(n)]
+                s_re = [sig_wave[d, re_at, :] for d in range(n)]
+                s_im = [sig_wave[d, im_at, :] for d in range(n)]
+                rows = []
+                for i in range(n):
+                    re = im = None
+                    for j in range(i + 1):
+                        a, b, x, y = f_re[i - j], f_im[i - j], s_re[j], s_im[j]
+                        re = a * x - b * y if re is None else re + a * x - b * y
+                        im = a * y + b * x if im is None else im + a * y + b * x
+                    rows.append((re, im))
+                done.append(rows)
+            re_at = pl.ds(pl.multiple_of(r * step, step), step)
+            im_at = pl.ds(pl.multiple_of(tok + r * step, step), step)
+            for i in range(n):
+                at = slice((i % 2) * lanes, (i % 2 + 1) * lanes)
+                for which, rows_at in enumerate((re_at, im_at)):
+                    whole = jnp.concatenate([done[0][i][which], done[1][i][which]], axis=0)
+                    out_wave[i // 2, rows_at, at] = whole.astype(BF16)
+            return 0
+
+        lax.fori_loop(0, tok // step, one, 0)
+
+    def return_chunk(c):
+        gain = gain_ref[:, chunk_lanes(c)]
+
+        def one(i, _):
+            x = pairs - 1 - i
+            couple = lax.div(met(2 * x), 2)
+            both = jnp.dot(back_ref[...], out_wave[couple], preferred_element_type=F32)
+            for k in range(2):
+                sig = recv[c, 2 * couple + k].astype(F32)
+                recv[c, 2 * couple + k] = (both[:, k * lanes : (k + 1) * lanes] + gain * sig).astype(BF16)
+
+            @pl.when(x > 0)
+            def _():
+                out_copy(c, 2 * x).start()
+
+            out_copy(c, 2 * x + 1).start()
+            return 0
+
+        lax.fori_loop(0, pairs, one, 0)
+
+    def q_turn(p, turned):
+        both = across(eye[:tok, :tok], q_ref[p].reshape(chunks * lanes, tok))
+        for c in range(chunks):
+            turned[c, SLOT:, :] = both[:, chunk_lanes(c)]
+            turned[c, :SLOT, :] = q_halo[p, :, chunk_lanes(c)].astype(F32)
+
+    def q_sums(p, turned):
+        for c in range(chunks):
+            taps = taps_ref[0, :, peer_rows(p, c)]
+            for start in range(0, tok, part):
+                q_rows[c, p, start : start + part, :] = sums_of(turned, (c,), taps, start, part).astype(BF16)
+
+    def q_range(first, last):
+        q_turn(first, turned_a)
+
+        def one(i, _):
+            p = first + 2 * i
+            q_turn(p + 1, turned_b)
+            q_sums(p, turned_a)
+            q_turn(lax.rem(p + 2, n), turned_a)
+            q_sums(p + 1, turned_b)
+            return 0
+
+        lax.fori_loop(0, (last - first) // 2, one, 0)
+
+    def mix(ref, peer, c):
+        mixed = (q_rows[c, peer].astype(F32) * ref[c, peer].astype(F32)).astype(BF16)
+        out_ref[peer_rows(peer, c), :] = across(eye[:lanes, :lanes], mixed).astype(BF16)
+
+    def mix_arrived(c, m):
+        out_copy(c, m).wait_recv()
+        mix(ret, met(m), c)
+
+    def mix_chunk(c):
+        mix(recv, me, c)
+        mix_arrived(c, jnp.int32(1))
+
+        def one(i, _):
+            x = pairs - 1 - i
+            mix_arrived(c, 2 * x)
+            mix_arrived(c, 2 * x + 1)
+            return 0
+
+        lax.fori_loop(0, pairs - 1, one, 0)
+
+    gate_chunk(0)
+    for i in range(1, len(side)):
+        side[i].wait()
+    for d in range(n):
+        filter_wave(d)
+    halo_wait(0)
+    lax.fori_loop(0, n, rim_step, 0, unroll=2)
+
+    def rim_starts(m, _):
+        rim_start(m)
+        return 0
+
+    lax.fori_loop(1, n, rim_starts, 0)
+    own_in(0).start()
+    for c in range(1, chunks):
+        gate_chunk(c)
+        own_in(c).start()
+    load_q.wait()
+    find_q_tails()
+    halo_start(1)
+    for c in range(chunks):
+        sig_chunk(c)
+        blend(c)
+        return_chunk(c)
+        if c == 0:
+            halo_wait(1)
+        q_range(c * n // chunks, (c + 1) * n // chunks)
+    for c in range(chunks):
+        mix_chunk(c)
+    await_bytes(gated.at[:, 0 : n - 1], in_send)
+    await_bytes(recv.at[:, 0 : n - 1], out_send)
 
 
 def kernel(
@@ -339,6 +759,67 @@
         lax.fori_loop(0, n, put_step, 0)
 
 
+def wide_call(n, queries, keys, values, taps, filters, gain):
+    width, tok = queries.shape
+    chan, length = filters.shape
+    chunks = chan // LANES
+    reach = taps.shape[1]
+    dma = pltpu.SemaphoreType.DMA
+    there, back = wave_tables(tok)
+    cut = [x.reshape(n, chunks, LANES, tok) for x in (queries, keys, values)]
+    held = [
+        pltpu.with_memory_space_constraint(x, pltpu.HBM)
+        for x in (*cut, taps, filters, gain, jnp.asarray(there), jnp.asarray(back))
+    ]
+    return pl.pallas_call(
+        functools.partial(wide_kernel, n),
+        out_shape=pltpu.VMEM((width, tok), BF16),
+        in_specs=[pl.BlockSpec(memory_space=pltpu.HBM)] * 8,
+        out_specs=pl.BlockSpec(memory_space=pltpu.VMEM),
+        scratch_shapes=[
+            pltpu.VMEM((n, chunks, LANES, tok), BF16),
+            pltpu.VMEM((chunks, n, 2, LANES, tok), BF16),
+            pltpu.VMEM((3, reach, width), F32),
+            pltpu.VMEM((chan, length), BF16),
+            pltpu.VMEM((1, chan), F32),
+            pltpu.VMEM(there.shape, BF16),
+            pltpu.VMEM(back.shape, BF16),
+            pltpu.VMEM((tok, tok), BF16),
+            pltpu.VMEM((chunks, n, SLOT, 2 * LANES), BF16),
+            pltpu.VMEM((chunks, n, SLOT, 2 * LANES), BF16),
+            pltpu.VMEM((n, SLOT, chan), BF16),
+            pltpu.VMEM((n, SLOT, chan), BF16),
+            pltpu.VMEM((2, SLOT + tok, LANES), F32),
+            pltpu.VMEM((2, SLOT + tok, LANES), F32),
+            pltpu.VMEM((2, n, SLOT + 16, LANES), F32),
+            pltpu.VMEM((chunks, n, tok, LANES), BF16),
+            pltpu.VMEM((chunks, n, tok, LANES), BF16),
+            pltpu.VMEM((chunks, n, tok, LANES), BF16),
+            pltpu.VMEM((chunks, n, tok, LANES), BF16),
+            pltpu.VMEM((2, 2 * tok, chan), F32),
+            pltpu.VMEM((chunks, n, 2 * tok, LANES), F32),
+            pltpu.VMEM((n, 2 * tok, LANES), F32),
+            pltpu.VMEM((n // 2, 2 * tok, 2 * LANES), BF16),
+            dma((n,)),
+            dma((chunks, 2)),
+            dma,
+            dma((5,)),
+            dma((2,)),
+            dma((2,)),
+            dma,
+            dma,
+            dma((chunks, n // 2)),
+            dma((chunks,)),
+            dma,
+            dma((chunks, n)),
+        ],
+        compiler_params=pltpu.CompilerParams(
+            collective_id=0, has_side_effects=True, vmem_limit_bytes=40 * 2**20
+        ),
+        name="hyena",
+    )(*held)
+
+
 def solution(mesh):
     n = mesh.shape["ctx"]
 
@@ -348,6 +829,8 @@
         blocks = length // LANES
         lanes = min(chan, LANES)
         chunks = chan // lanes
+        if n in (4, 8) and chan == 2 * LANES and tok == 2 * LANES and length == n * tok and width == n * chan:
+            return wide_call(n, queries, keys, values, short_taps, long_filter[0], skip_gain)
         table = jnp.asarray(circle_tables())
         twist = jnp.asarray(twist_columns(blocks))
         dma = pltpu.SemaphoreType.DMA

time: 38 us -> 32.5 us (0.86)
  Pallas kernels: 35.6 us -> 31.4 us
  local copies, waits for them, and re-layouts: 2.26 us -> 0.97 us
    pallas_call x1, Pallas kernels: 35.6 us -> 31.4 us  [wide_call(): pl.pallas_call(functools.partial(wide_kernel, n), out_shape=pltpu.VMEM((w...]
    unnamed x1, local copies, waits for them, and re-layouts: 2.26 us -> 0.97 us
where the time goes in v3:
time: 32.5 us; the launch traced here: 32.4 us
  Pallas kernels  31.4 us (97%)
  local copies, waits for them, and re-layouts  0.97 us (3%)
    pallas_call x1, Pallas kernels, wide_call(): pl.pallas_call(functools.partial(wide_kernel, n), out_shape=pltpu.VMEM((w...  31.4 us
    unnamed x1, local copies, waits for them, and re-layouts  0.97 us

profile of v3, /device:TPU:0, one launch (start us, length us, event | category | flops | bytes accessed | tf_op | source)
XLA Modules:
  0.0 32.4 jit_solution(9096942429130544411)
XLA Ops:
  0.0 31.4 %hyena.1 = bf16[2048,256]{1,0:T(8,128)(2,1)S(1)} custom-call(bf16[8,2,128,256]{3,2,1,0:T(8,128)(2,1)} %bitcast.4, bf16[8,2,128,256]{3,2,1,0:T(8,128)(2,1)} %bitcast.5, bf16[8,2,128,256]{3,2,1,0:T(8,128)(2,1)} %bitcast.6, f32[3,7,2048]{2,1,0:T(8,128)} %taps_hbm.1, bf16[256,2048]{1,0:T(8,128)(2,1)} %bitcast.7, f32[1,256]{1,0:T(1,128)} %gain_hbm.1, ...), custom_call_target="tpu_custom_call" | custom-call | tf_op jit(solution)/shard_map/hyena/pallas_call | solution.py:774
  31.4 1.0 %copy.10 = bf16[2048,256]{1,0:T(8,128)(2,1)} copy(bf16[2048,256]{1,0:T(8,128)(2,1)S(1)} %hyena.1) | data formatting | bytes 2097152

commit v4 on v3

--- a/solution.py
+++ b/solution.py
@@ -89,7 +89,7 @@
 
 
 def wave_tables(tok):
-    bins = np.concatenate([np.arange(0, tok, 2), np.arange(1, tok, 2)])
+    bins = np.arange(tok).reshape(-1, SLOT, 2).transpose(0, 2, 1).reshape(-1)
     angle = (2 * bins + 1)[:, None] * np.arange(tok)[None, :] * (math.pi / (2 * tok))
     there = np.concatenate([np.cos(angle), np.sin(angle)], axis=0)
     return there.astype(ml_dtypes.bfloat16), (there.T / tok).astype(ml_dtypes.bfloat16)
@@ -97,7 +97,7 @@
 
 def send_order(n):
     pairs = [(m, m - 1) for m in range(n - 1, 0, -2)]
-    return [(4, 2), (5, 3), (6, 7), (1, 0)] if n == 8 else pairs
+    return [(4, 6), (2, 7), (5, 3), (1, 0)] if n == 8 else pairs
 
 
 def wide_kernel(
@@ -186,7 +186,7 @@
         q_halo[...] = jnp.zeros_like(q_halo)
 
     def halo_copy(which):
-        mine, theirs = ((tails, halo), (q_tails, q_halo))[which]
+        mine, theirs = (tails.at[which], halo.at[which]) if which < chunks else (q_tails, q_halo)
         return pltpu.make_async_remote_copy(
             src_ref=mine, dst_ref=theirs, send_sem=halo_send.at[which], recv_sem=halo_recv.at[which],
             device_id={"ctx": lax.rem(me + 1, n)}, device_id_type=MESH,
@@ -206,14 +206,13 @@
         def _():
             halo_copy(which).wait_recv()
 
-    def find_tails():
-        for c in range(chunks):
-            def one(p, _):
-                block = source[c, p].reshape(2 * lanes, tok)
-                tails[c, p] = across(pick, block[:, tok - LANES :]).astype(BF16)
-                return 0
-
-            lax.fori_loop(0, n, one, 0, unroll=4)
+    def find_tails(c):
+        def one(p, _):
+            block = source[c, p].reshape(2 * lanes, tok)
+            tails[c, p] = across(pick, block[:, tok - LANES :]).astype(BF16)
+            return 0
+
+        lax.fori_loop(0, n, one, 0, unroll=4)
 
     def find_q_tails():
         def one(p, _):
@@ -267,7 +266,7 @@
         peer = met(m)
         pltpu.make_async_remote_copy(
             src_ref=gated.at[0, peer, 0:edge, :], dst_ref=recv.at[0, me, 0:edge, :],
-            send_sem=in_send, recv_sem=rim_recv,
+            send_sem=in_send, recv_sem=rim_recv.at[lax.div(m, 2)],
             device_id={"ctx": peer}, device_id_type=MESH,
         ).start()
 
@@ -291,55 +290,51 @@
                 load_wait(jnp.int32(m))
             side[0].wait()
         turn(c, jnp.int32(order[0][0]), turned_a)
-        if c == 0:
-            pl.semaphore_wait(barrier, n - 1)
 
         def one(i, codes):
             a, b = lax.rem(codes[0], n), lax.rem(codes[1], n)
             codes = (lax.div(codes[0], n), lax.div(codes[1], n))
             after = lax.rem(codes[0], n)
+            turn(c, b, turned_b)
+            gate(c, a, turned_a)
             if c == 0:
-                @pl.when(i == 1)
+                @pl.when(i == 0)
+                def _():
+                    pl.semaphore_wait(barrier, n - 1)
+
+            in_start(c, a)
+            turn(c, after, turned_a)
+            gate(c, b, turned_b)
+
+            @pl.when(i < pairs - 1)
+            def _():
+                in_start(c, b)
+
+            if c == 0:
+                @pl.when(i == 0)
                 def _():
                     for m in (order[1][1], *(m for pair in order[2:] for m in pair)):
                         load_wait(jnp.int32(m))
+                    find_tails(0)
+                    halo_start(0)
+
+                @pl.when(i == 1)
+                def _():
                     for k in range(1, chunks):
                         for copy in rest(k):
                             copy.wait()
-                    find_tails()
-                    halo_start(0)
-
-            turn(c, b, turned_b)
-            gate(c, a, turned_a)
-            in_start(c, a)
-            turn(c, after, turned_a)
-            gate(c, b, turned_b)
-
-            @pl.when(i < pairs - 1)
-            def _():
-                in_start(c, b)
+                        find_tails(k)
+                        halo_start(k)
 
             return codes
 
         lax.fori_loop(0, pairs, one, (jnp.int32(first_code), jnp.int32(second_code)))
 
-    def filter_wave(d):
-        wave[d % 2] = across(there_ref[...], filt_ref[:, d * tok : (d + 1) * tok])
-        now, before = wave.at[d % 2], wave.at[1 - d % 2]
-
-        def one(r, _):
-            for first, sign in ((0, 1.0), (tok // 2, -1.0)):
-                re_at = pl.ds(pl.multiple_of(first + r * step, step), step)
-                im_at = pl.ds(pl.multiple_of(tok + first + r * step, step), step)
-                re, im = now[re_at, :], now[im_at, :]
-                if d > 0:
-                    re, im = re + sign * before[im_at, :], im - sign * before[re_at, :]
-                for c in range(chunks):
-                    filt_wave[c, d, re_at, :] = re[:, chunk_lanes(c)]
-                    filt_wave[c, d, im_at, :] = im[:, chunk_lanes(c)]
-            return 0
-
-        lax.fori_loop(0, tok // 2 // step, one, 0, unroll=2)
+    def filter_range(first, last):
+        for d in range(first, last):
+            both = across(there_ref[...], filt_ref[:, d * tok : (d + 1) * tok])
+            for c in range(chunks):
+                filt_wave[c, d] = both[:, chunk_lanes(c)]
 
     def rim_step(p, _):
         sums = []
@@ -357,15 +352,17 @@
 
     def sig_chunk(c):
         at = slice(0 if c else edge, tok)
-        if c == 0:
-            await_bytes(recv.at[0, 0 : n - 1, 0:edge, :], rim_recv)
         own_in(c).wait()
         await_bytes(recv.at[c, met(jnp.int32(1)), at, :], in_recv.at[c, 0])
+        if c == 0:
+            await_bytes(recv.at[c, met(jnp.int32(1)), 0:edge, :], rim_recv.at[0])
         sig_couple(c, 2 * lax.div(me, 2))
 
         def one(x, _):
             first = 2 * lax.div(met(2 * x), 2)
             await_bytes(recv.at[c, pl.ds(first, 2), at, :], in_recv.at[c, x])
+            if c == 0:
+                await_bytes(recv.at[c, pl.ds(first, 2), 0:edge, :], rim_recv.at[x])
             sig_couple(c, first)
             return 0
 
@@ -382,14 +379,20 @@
                 f_im = [filt_wave[c, d, im_at, :] for d in range(n)]
                 s_re = [sig_wave[d, re_at, :] for d in range(n)]
                 s_im = [sig_wave[d, im_at, :] for d in range(n)]
-                rows = []
+                rows, past = [], None
                 for i in range(n):
                     re = im = None
                     for j in range(i + 1):
                         a, b, x, y = f_re[i - j], f_im[i - j], s_re[j], s_im[j]
                         re = a * x - b * y if re is None else re + a * x - b * y
                         im = a * y + b * x if im is None else im + a * y + b * x
-                    rows.append((re, im))
+                    if past is None:
+                        rows.append((re, im))
+                    elif part_of == 0:
+                        rows.append((re + past[1], im - past[0]))
+                    else:
+                        rows.append((re - past[1], im + past[0]))
+                    past = (re, im)
                 done.append(rows)
             re_at = pl.ds(pl.multiple_of(r * step, step), step)
             im_at = pl.ds(pl.multiple_of(tok + r * step, step), step)
@@ -405,22 +408,27 @@
     def return_chunk(c):
         gain = gain_ref[:, chunk_lanes(c)]
 
-        def one(i, _):
-            x = pairs - 1 - i
-            couple = lax.div(met(2 * x), 2)
-            both = jnp.dot(back_ref[...], out_wave[couple], preferred_element_type=F32)
+        def couple_of(x):
+            return lax.div(met(2 * x), 2)
+
+        def invert(x, slot):
+            wave[slot] = jnp.dot(back_ref[...], out_wave[couple_of(x)], preferred_element_type=F32)
+
+        def finish(x, slot):
             for k in range(2):
-                sig = recv[c, 2 * couple + k].astype(F32)
-                recv[c, 2 * couple + k] = (both[:, k * lanes : (k + 1) * lanes] + gain * sig).astype(BF16)
-
-            @pl.when(x > 0)
-            def _():
+                p = 2 * couple_of(x) + k
+                both = wave[slot, :, k * lanes : (k + 1) * lanes]
+                recv[c, p] = (both + gain * recv[c, p].astype(F32)).astype(BF16)
+
+        invert(jnp.int32(pairs - 1), 0)
+        for i in range(pairs):
+            x = jnp.int32(pairs - 1 - i)
+            if i < pairs - 1:
+                invert(x - 1, (i + 1) % 2)
+            finish(x, i % 2)
+            if i < pairs - 1:
                 out_copy(c, 2 * x).start()
-
             out_copy(c, 2 * x + 1).start()
-            return 0
-
-        lax.fori_loop(0, pairs, one, 0)
 
     def q_turn(p, turned):
         both = across(eye[:tok, :tok], q_ref[p].reshape(chunks * lanes, tok))
@@ -470,8 +478,8 @@
     gate_chunk(0)
     for i in range(1, len(side)):
         side[i].wait()
-    for d in range(n):
-        filter_wave(d)
+    early = (3 * n) // 8
+    filter_range(0, early)
     halo_wait(0)
     lax.fori_loop(0, n, rim_step, 0, unroll=2)
 
@@ -482,17 +490,19 @@
     lax.fori_loop(1, n, rim_starts, 0)
     own_in(0).start()
     for c in range(1, chunks):
+        halo_wait(c)
         gate_chunk(c)
         own_in(c).start()
+    filter_range(early, n)
     load_q.wait()
     find_q_tails()
-    halo_start(1)
+    halo_start(chunks)
     for c in range(chunks):
         sig_chunk(c)
         blend(c)
         return_chunk(c)
         if c == 0:
-            halo_wait(1)
+            halo_wait(chunks)
         q_range(c * n // chunks, (c + 1) * n // chunks)
     for c in range(chunks):
         mix_chunk(c)
@@ -796,7 +806,7 @@
             pltpu.VMEM((chunks, n, tok, LANES), BF16),
             pltpu.VMEM((chunks, n, tok, LANES), BF16),
             pltpu.VMEM((chunks, n, tok, LANES), BF16),
-            pltpu.VMEM((2, 2 * tok, chan), F32),
+            pltpu.VMEM((2, tok, 2 * LANES), F32),
             pltpu.VMEM((chunks, n, 2 * tok, LANES), F32),
             pltpu.VMEM((n, 2 * tok, LANES), F32),
             pltpu.VMEM((n // 2, 2 * tok, 2 * LANES), BF16),
@@ -804,9 +814,9 @@
             dma((chunks, 2)),
             dma,
             dma((5,)),
-            dma((2,)),
-            dma((2,)),
-            dma,
+            dma((chunks + 1,)),
+            dma((chunks + 1,)),
+            dma((n // 2,)),
             dma,
             dma((chunks, n // 2)),
             dma((chunks,)),

time: 32.5 us -> 30.7 us (0.945)
  Pallas kernels: 31.4 us -> 29.6 us
    pallas_call x1, Pallas kernels: 31.4 us -> 29.6 us  [wide_call(): pl.pallas_call(functools.partial(wide_kernel, n), out_shape=pltpu.VMEM((w...]
where the time goes in v4:
time: 30.7 us; the launch traced here: 30.6 us
  Pallas kernels  29.6 us (96%)
  local copies, waits for them, and re-layouts  0.97 us (3%)
    pallas_call x1, Pallas kernels, wide_call(): pl.pallas_call(functools.partial(wide_kernel, n), out_shape=pltpu.VMEM((w...  29.6 us
    unnamed x1, local copies, waits for them, and re-layouts  0.97 us

profile of v4, /device:TPU:0, one launch (start us, length us, event | category | flops | bytes accessed | tf_op | source)
XLA Modules:
  0.0 30.6 jit_solution(16917198437604290376)
XLA Ops:
  0.0 29.6 %hyena.1 = bf16[2048,256]{1,0:T(8,128)(2,1)S(1)} custom-call(bf16[8,2,128,256]{3,2,1,0:T(8,128)(2,1)} %bitcast.4, bf16[8,2,128,256]{3,2,1,0:T(8,128)(2,1)} %bitcast.5, bf16[8,2,128,256]{3,2,1,0:T(8,128)(2,1)} %bitcast.6, f32[3,7,2048]{2,1,0:T(8,128)} %taps_hbm.1, bf16[256,2048]{1,0:T(8,128)(2,1)} %bitcast.7, f32[1,256]{1,0:T(1,128)} %gain_hbm.1, ...), custom_call_target="tpu_custom_call" | custom-call | tf_op jit(solution)/shard_map/hyena/pallas_call | solution.py:784
  29.6 1.0 %copy.10 = bf16[2048,256]{1,0:T(8,128)(2,1)} copy(bf16[2048,256]{1,0:T(8,128)(2,1)S(1)} %hyena.1) | data formatting | bytes 2097152

commit v5 on v4

--- a/solution.py
+++ b/solution.py
@@ -97,7 +97,7 @@
 
 def send_order(n):
     pairs = [(m, m - 1) for m in range(n - 1, 0, -2)]
-    return [(4, 6), (2, 7), (5, 3), (1, 0)] if n == 8 else pairs
+    return [(6, 7), (4, 2), (5, 3), (1, 0)] if n == 8 else pairs
 
 
 def wide_kernel(
@@ -105,7 +105,7 @@
     q_hbm, k_hbm, v_hbm, taps_hbm, filt_hbm, gain_hbm, there_hbm, back_hbm,
     out_ref,
     q_ref, source, taps_ref, filt_ref, gain_ref, there_ref, back_ref,
-    eye, tails, halo, q_tails, q_halo, turned_a, turned_b, rim, gated, recv, ret, q_rows,
+    eye, tails, halo, q_tails, q_halo, turned_a, turned_b, rim, gated, recv, ret, sent,
     wave, filt_wave, sig_wave, out_wave,
     load_sem, rest_sem, q_sem, side_sem, halo_send, halo_recv,
     rim_recv, in_send, in_recv, in_own, out_send, out_recv,
@@ -119,6 +119,7 @@
     edge = 16
     part = 64
     order = send_order(n)
+    couples = [2, 1, 3, 0] if n == 8 else list(range(pairs - 1, -1, -1))
     first_code = sum(a * n**i for i, (a, _) in enumerate(order))
     second_code = sum(b * n**i for i, (_, b) in enumerate(order))
 
@@ -276,7 +277,7 @@
     def out_copy(c, m):
         peer = met(m)
         return pltpu.make_async_remote_copy(
-            src_ref=recv.at[c, peer], dst_ref=ret.at[c, me],
+            src_ref=sent.at[c, peer], dst_ref=ret.at[c, me],
             send_sem=out_send, recv_sem=out_recv.at[c, m],
             device_id={"ctx": peer}, device_id_type=MESH,
         )
@@ -418,17 +419,17 @@
             for k in range(2):
                 p = 2 * couple_of(x) + k
                 both = wave[slot, :, k * lanes : (k + 1) * lanes]
-                recv[c, p] = (both + gain * recv[c, p].astype(F32)).astype(BF16)
-
-        invert(jnp.int32(pairs - 1), 0)
-        for i in range(pairs):
-            x = jnp.int32(pairs - 1 - i)
+                rows = (both + gain * recv[c, p].astype(F32)).astype(BF16)
+                sent[c, p] = across(eye[:lanes, :lanes], rows).astype(BF16)
+
+        invert(jnp.int32(couples[0]), 0)
+        for i, x in enumerate(couples):
             if i < pairs - 1:
-                invert(x - 1, (i + 1) % 2)
-            finish(x, i % 2)
-            if i < pairs - 1:
-                out_copy(c, 2 * x).start()
-            out_copy(c, 2 * x + 1).start()
+                invert(jnp.int32(couples[i + 1]), (i + 1) % 2)
+            finish(jnp.int32(x), i % 2)
+            if x > 0:
+                out_copy(c, jnp.int32(2 * x)).start()
+            out_copy(c, jnp.int32(2 * x + 1)).start()
 
     def q_turn(p, turned):
         both = across(eye[:tok, :tok], q_ref[p].reshape(chunks * lanes, tok))
@@ -439,8 +440,8 @@
     def q_sums(p, turned):
         for c in range(chunks):
             taps = taps_ref[0, :, peer_rows(p, c)]
-            for start in range(0, tok, part):
-                q_rows[c, p, start : start + part, :] = sums_of(turned, (c,), taps, start, part).astype(BF16)
+            rows = [sums_of(turned, (c,), taps, start, part).astype(BF16) for start in range(0, tok, part)]
+            out_ref[peer_rows(p, c), :] = across(eye[:lanes, :lanes], jnp.concatenate(rows, axis=0)).astype(BF16)
 
     def q_range(first, last):
         q_turn(first, turned_a)
@@ -456,24 +457,21 @@
         lax.fori_loop(0, (last - first) // 2, one, 0)
 
     def mix(ref, peer, c):
-        mixed = (q_rows[c, peer].astype(F32) * ref[c, peer].astype(F32)).astype(BF16)
-        out_ref[peer_rows(peer, c), :] = across(eye[:lanes, :lanes], mixed).astype(BF16)
+        at = peer_rows(peer, c)
+        out_ref[at, :] = (out_ref[at, :].astype(F32) * ref[c, peer].astype(F32)).astype(BF16)
 
     def mix_arrived(c, m):
         out_copy(c, m).wait_recv()
         mix(ret, met(m), c)
 
     def mix_chunk(c):
-        mix(recv, me, c)
+        mix(sent, me, c)
         mix_arrived(c, jnp.int32(1))
 
-        def one(i, _):
-            x = pairs - 1 - i
-            mix_arrived(c, 2 * x)
-            mix_arrived(c, 2 * x + 1)
-            return 0
-
-        lax.fori_loop(0, pairs - 1, one, 0)
+        for x in couples:
+            if x > 0:
+                mix_arrived(c, jnp.int32(2 * x))
+                mix_arrived(c, jnp.int32(2 * x + 1))
 
     gate_chunk(0)
     for i in range(1, len(side)):
@@ -507,7 +505,7 @@
     for c in range(chunks):
         mix_chunk(c)
     await_bytes(gated.at[:, 0 : n - 1], in_send)
-    await_bytes(recv.at[:, 0 : n - 1], out_send)
+    await_bytes(sent.at[:, 0 : n - 1], out_send)
 
 
 def kernel(
@@ -804,8 +802,8 @@
             pltpu.VMEM((2, n, SLOT + 16, LANES), F32),
             pltpu.VMEM((chunks, n, tok, LANES), BF16),
             pltpu.VMEM((chunks, n, tok, LANES), BF16),
-            pltpu.VMEM((chunks, n, tok, LANES), BF16),
-            pltpu.VMEM((chunks, n, tok, LANES), BF16),
+            pltpu.VMEM((chunks, n, LANES, tok), BF16),
+            pltpu.VMEM((chunks, n, LANES, tok), BF16),
             pltpu.VMEM((2, tok, 2 * LANES), F32),
             pltpu.VMEM((chunks, n, 2 * tok, LANES), F32),
             pltpu.VMEM((n, 2 * tok, LANES), F32),

time: 30.7 us -> 29.9 us (0.974)
  Pallas kernels: 29.6 us -> 28.8 us
    pallas_call x1, Pallas kernels: 29.6 us -> 28.8 us  [wide_call(): pl.pallas_call(functools.partial(wide_kernel, n), out_shape=pltpu.VMEM((w...]
where the time goes in v5:
time: 29.9 us; the launch traced here: 29.8 us
  Pallas kernels  28.8 us (96%)
  local copies, waits for them, and re-layouts  0.97 us (3%)
    pallas_call x1, Pallas kernels, wide_call(): pl.pallas_call(functools.partial(wide_kernel, n), out_shape=pltpu.VMEM((w...  28.8 us
    unnamed x1, local copies, waits for them, and re-layouts  0.97 us

profile of v5, /device:TPU:0, one launch (start us, length us, event | category | flops | bytes accessed | tf_op | source)
XLA Modules:
  0.0 29.8 jit_solution(16816828875910113375)
XLA Ops:
  0.0 28.8 %hyena.1 = bf16[2048,256]{1,0:T(8,128)(2,1)S(1)} custom-call(bf16[8,2,128,256]{3,2,1,0:T(8,128)(2,1)} %bitcast.4, bf16[8,2,128,256]{3,2,1,0:T(8,128)(2,1)} %bitcast.5, bf16[8,2,128,256]{3,2,1,0:T(8,128)(2,1)} %bitcast.6, f32[3,7,2048]{2,1,0:T(8,128)} %taps_hbm.1, bf16[256,2048]{1,0:T(8,128)(2,1)} %bitcast.7, f32[1,256]{1,0:T(1,128)} %gain_hbm.1, ...), custom_call_target="tpu_custom_call" | custom-call | tf_op jit(solution)/shard_map/hyena/pallas_call | solution.py:782
  28.8 1.0 %copy.10 = bf16[2048,256]{1,0:T(8,128)(2,1)} copy(bf16[2048,256]{1,0:T(8,128)(2,1)S(1)} %hyena.1) | data formatting | bytes 2097152

commit v6 on v5

--- a/solution.py
+++ b/solution.py
@@ -124,22 +124,28 @@
     second_code = sum(b * n**i for i, (_, b) in enumerate(order))
 
     barrier = pltpu.get_barrier_semaphore()
-    for d in range(1, n):
-        pl.semaphore_signal(
-            barrier, inc=1, device_id={"ctx": lax.rem(me + d, n)}, device_id_type=MESH
-        )
+    beside = me + 1 - 2 * lax.rem(me, 2)
+    pair = me - lax.rem(me, 2)
+    for peer in (n - 1 - me, n - 1 - beside):
+        pl.semaphore_signal(barrier, inc=1, device_id={"ctx": peer}, device_id_type=MESH)
+    for x in range(2, n - 2, 2):
+        for peer in (crossed(me, jnp.int32(x), n), crossed(beside, jnp.int32(x), n)):
+            pl.semaphore_signal(barrier, inc=1, device_id={"ctx": peer}, device_id_type=MESH)
+    pl.semaphore_signal(barrier, inc=1, device_id={"ctx": beside}, device_id_type=MESH)
 
     def met(m):
         return crossed(me, m, n)
 
-    def load_start(m):
-        p = met(m)
+    needed = [m for pair in order for m in pair]
+
+    def load_start(m, slot):
+        p = met(jnp.int32(m))
         for w, ref in enumerate((k_hbm, v_hbm)):
-            pltpu.make_async_copy(ref.at[p, 0], source.at[0, p, w], load_sem.at[m]).start()
-
-    def load_wait(m):
-        p = met(m)
-        pltpu.make_async_copy(source.at[0, p], source.at[0, p], load_sem.at[m]).wait()
+            pltpu.make_async_copy(ref.at[p, 0], source.at[0, p, w], load_sem.at[slot]).start()
+
+    def load_wait(m, slot):
+        p = met(jnp.int32(m))
+        pltpu.make_async_copy(source.at[0, p], source.at[0, p], load_sem.at[slot]).wait()
 
     def rest(c):
         return [
@@ -156,10 +162,9 @@
     ]
     load_q = pltpu.make_async_copy(q_hbm, q_ref, q_sem)
 
-    for i, (a, b) in enumerate(order):
-        load_start(jnp.int32(a))
-        load_start(jnp.int32(b))
-        if i == 0:
+    for i, m in enumerate(needed):
+        load_start(m, min(i, 3))
+        if i == 1:
             side[0].start()
     for c in range(1, chunks):
         for copy in rest(c):
@@ -278,7 +283,7 @@
         peer = met(m)
         return pltpu.make_async_remote_copy(
             src_ref=sent.at[c, peer], dst_ref=ret.at[c, me],
-            send_sem=out_send, recv_sem=out_recv.at[c, m],
+            send_sem=out_send, recv_sem=out_recv.at[0 if c == 0 else (c - 1) * (n - 1) + m],
             device_id={"ctx": peer}, device_id_type=MESH,
         )
 
@@ -287,8 +292,8 @@
 
     def gate_chunk(c):
         if c == 0:
-            for m in (*order[0], order[1][0]):
-                load_wait(jnp.int32(m))
+            for i, m in enumerate(needed[:3]):
+                load_wait(m, i)
             side[0].wait()
         turn(c, jnp.int32(order[0][0]), turned_a)
 
@@ -314,8 +319,7 @@
             if c == 0:
                 @pl.when(i == 0)
                 def _():
-                    for m in (order[1][1], *(m for pair in order[2:] for m in pair)):
-                        load_wait(jnp.int32(m))
+                    await_bytes(source.at[0, 0 : n - 3], load_sem.at[3])
                     find_tails(0)
                     halo_start(0)
 
@@ -461,11 +465,14 @@
         out_ref[at, :] = (out_ref[at, :].astype(F32) * ref[c, peer].astype(F32)).astype(BF16)
 
     def mix_arrived(c, m):
-        out_copy(c, m).wait_recv()
+        if c > 0:
+            out_copy(c, m).wait_recv()
         mix(ret, met(m), c)
 
     def mix_chunk(c):
         mix(sent, me, c)
+        if c == 0:
+            await_bytes(ret.at[0, 0 : n - 1], out_recv.at[0])
         mix_arrived(c, jnp.int32(1))
 
         for x in couples:
@@ -808,7 +815,7 @@
             pltpu.VMEM((chunks, n, 2 * tok, LANES), F32),
             pltpu.VMEM((n, 2 * tok, LANES), F32),
             pltpu.VMEM((n // 2, 2 * tok, 2 * LANES), BF16),
-            dma((n,)),
+            dma((4,)),
             dma((chunks, 2)),
             dma,
             dma((5,)),
@@ -819,7 +826,7 @@
             dma((chunks, n // 2)),
             dma((chunks,)),
             dma,
-            dma((chunks, n)),
+            dma(((chunks - 1) * (n - 1) + 1,)),
         ],
         compiler_params=pltpu.CompilerParams(
             collective_id=0, has_side_effects=True, vmem_limit_bytes=40 * 2**20

time: 29.9 us -> 29.8 us (level)
  no operation moved by 1% of the time
where the time goes in v6:
time: 29.8 us; the launch traced here: 29.6 us
  Pallas kernels  28.7 us (96%)
  local copies, waits for them, and re-layouts  0.97 us (3%)
    pallas_call x1, Pallas kernels, wide_call(): pl.pallas_call(functools.partial(wide_kernel, n), out_shape=pltpu.VMEM((w...  28.7 us
    unnamed x1, local copies, waits for them, and re-layouts  0.97 us

profile of v6, /device:TPU:0, one launch (start us, length us, event | category | flops | bytes accessed | tf_op | source)
XLA Modules:
  0.0 29.6 jit_solution(12541747202917643637)
XLA Ops:
  0.0 28.7 %hyena.1 = bf16[2048,256]{1,0:T(8,128)(2,1)S(1)} custom-call(bf16[8,2,128,256]{3,2,1,0:T(8,128)(2,1)} %bitcast.4, bf16[8,2,128,256]{3,2,1,0:T(8,128)(2,1)} %bitcast.5, bf16[8,2,128,256]{3,2,1,0:T(8,128)(2,1)} %bitcast.6, f32[3,7,2048]{2,1,0:T(8,128)} %taps_hbm.1, bf16[256,2048]{1,0:T(8,128)(2,1)} %bitcast.7, f32[1,256]{1,0:T(1,128)} %gain_hbm.1, ...), custom_call_target="tpu_custom_call" | custom-call | tf_op jit(solution)/shard_map/hyena/pallas_call | solution.py:789
  28.7 1.0 %copy.10 = bf16[2048,256]{1,0:T(8,128)(2,1)} copy(bf16[2048,256]{1,0:T(8,128)(2,1)S(1)} %hyena.1) | data formatting | bytes 2097152

commit v7 on v6

--- a/solution.py
+++ b/solution.py
@@ -120,8 +120,10 @@
     part = 64
     order = send_order(n)
     couples = [2, 1, 3, 0] if n == 8 else list(range(pairs - 1, -1, -1))
-    first_code = sum(a * n**i for i, (a, _) in enumerate(order))
-    second_code = sum(b * n**i for i, (_, b) in enumerate(order))
+    later = [(4, 2), (5, 3), (6, 7), (1, 0)] if n == 8 else order
+
+    def code_of(pairs_of, k):
+        return jnp.int32(sum(pair[k] * n**i for i, pair in enumerate(pairs_of)))
 
     barrier = pltpu.get_barrier_semaphore()
     beside = me + 1 - 2 * lax.rem(me, 2)
@@ -295,7 +297,7 @@
             for i, m in enumerate(needed[:3]):
                 load_wait(m, i)
             side[0].wait()
-        turn(c, jnp.int32(order[0][0]), turned_a)
+        turn(c, jnp.int32((later if c else order)[0][0]), turned_a)
 
         def one(i, codes):
             a, b = lax.rem(codes[0], n), lax.rem(codes[1], n)
@@ -333,7 +335,7 @@
 
             return codes
 
-        lax.fori_loop(0, pairs, one, (jnp.int32(first_code), jnp.int32(second_code)))
+        lax.fori_loop(0, pairs, one, (code_of(later if c else order, 0), code_of(later if c else order, 1)))
 
     def filter_range(first, last):
         for d in range(first, last):
@@ -509,9 +511,9 @@
         if c == 0:
             halo_wait(chunks)
         q_range(c * n // chunks, (c + 1) * n // chunks)
+    await_bytes(gated.at[:, 0 : n - 1], in_send)
     for c in range(chunks):
         mix_chunk(c)
-    await_bytes(gated.at[:, 0 : n - 1], in_send)
     await_bytes(sent.at[:, 0 : n - 1], out_send)
 
 

time: 29.8 us -> 29.8 us (level)
  no operation moved by 1% of the time
where the time goes in v7:
time: 29.8 us; the launch traced here: 29.6 us
  Pallas kernels  28.7 us (96%)
  local copies, waits for them, and re-layouts  0.97 us (3%)
    pallas_call x1, Pallas kernels, wide_call(): pl.pallas_call(functools.partial(wide_kernel, n), out_shape=pltpu.VMEM((w...  28.7 us
    unnamed x1, local copies, waits for them, and re-layouts  0.97 us

profile of v7, /device:TPU:0, one launch (start us, length us, event | category | flops | bytes accessed | tf_op | source)
XLA Modules:
  0.0 29.6 jit_solution(3142858880020978067)
XLA Ops:
  0.0 28.7 %hyena.1 = bf16[2048,256]{1,0:T(8,128)(2,1)S(1)} custom-call(bf16[8,2,128,256]{3,2,1,0:T(8,128)(2,1)} %bitcast.4, bf16[8,2,128,256]{3,2,1,0:T(8,128)(2,1)} %bitcast.5, bf16[8,2,128,256]{3,2,1,0:T(8,128)(2,1)} %bitcast.6, f32[3,7,2048]{2,1,0:T(8,128)} %taps_hbm.1, bf16[256,2048]{1,0:T(8,128)(2,1)} %bitcast.7, f32[1,256]{1,0:T(1,128)} %gain_hbm.1, ...), custom_call_target="tpu_custom_call" | custom-call | tf_op jit(solution)/shard_map/hyena/pallas_call | solution.py:791
  28.7 1.0 %copy.10 = bf16[2048,256]{1,0:T(8,128)(2,1)} copy(bf16[2048,256]{1,0:T(8,128)(2,1)S(1)} %hyena.1) | data formatting | bytes 2097152
